TPU v7x, 512 devices: a whole 4x4x16 slice. The times are simulated.
512 devices in a mesh: frame: 16 (over z_hi, x, core), tile: 32 (over z_lo, y).
Axes of the slice: x: 4, y: 4, z: 16 (z_hi: 2, z_lo: 8; z = z_hi * 8 + z_lo), core: 2. Of those that a mesh axis runs over, the one named last changes fastest.
Arguments:
- state_tokens: bfloat16 [16, 32768, 256], P('frame', 'tile'), may hold values from -12 to 12
- gain_time: float32 [256], replicated, may hold values from 0.25 to 1.75
- query_time: bfloat16 [256, 256], replicated, may hold values from -2 to 2
- key_time: bfloat16 [256, 256], replicated, may hold values from -2 to 2
- value_time: bfloat16 [256, 256], replicated, may hold values from -0.375 to 0.375
- output_time: bfloat16 [256, 256], replicated, may hold values from -0.375 to 0.375
- gain_space: float32 [256], replicated, may hold values from 0.25 to 1.75
- query_space: bfloat16 [256, 256], replicated, may hold values from -2 to 2
- key_space: bfloat16 [256, 256], replicated, may hold values from -2 to 2
- value_space: bfloat16 [256, 256], replicated, may hold values from -0.375 to 0.375
- output_space: bfloat16 [256, 256], replicated, may hold values from -0.375 to 0.375
- neighbours: int32 [256, 9], P('tile'), may hold values from -1 to 255, as said below
Outputs:
- updated: bfloat16 [16, 32768, 256], P('frame', 'tile')
Inputs may be any that keep to these rules, and one draw needn't show every extreme that they name: `neighbours`: entry 0 of row b is b itself; the other entries are distinct block ids at most 8 blocks away from b in the cyclic order of the 256 blocks, or -1; only the last entry is ever -1.
All inputs are finite; a program needn't handle non-finite values.
Results may differ from a plain program's by a relative error of at most 0.013.
Values may be sent and summed in bfloat16 or wider, within the bound.
A program may use at most 64 MiB of HBM per device.

v0:
```python
import jax
import jax.numpy as jnp
from jax import lax
from jax.sharding import PartitionSpec as P

HEADS = 8
BLOCK = 128
NEIGHBOUR_COUNT = 9


EPS = 1e-05
ROT_PERIOD = 1024


def padded(value, sides, width):
    for axis, dim in sides:
        count, length = (lax.axis_size(axis), value.shape[dim])
        up = [(i, (i + 1) % count) for i in range(count)]
        down = [(j, i) for i, j in up]
        last = lax.slice_in_dim(value, length - width, length, axis=dim)
        initial = lax.slice_in_dim(value, 0, width, axis=dim)
        before = lax.ppermute(last, axis, up)
        after = lax.ppermute(initial, axis, down)
        value = jnp.concatenate([before, value, after], axis=dim)
    return value


def rms_scale(rows, gain):
    values = rows.astype(jnp.float32)
    square_mean = jnp.mean(values * values, axis=-1, keepdims=True)
    return (values * lax.rsqrt(square_mean + EPS) * gain).astype(jnp.bfloat16)


def project_rows(rows, weight):
    flat = rows.reshape(-1, rows.shape[-1])
    result = jnp.dot(flat, weight, preferred_element_type=jnp.float32)
    return result.reshape(rows.shape[:-1] + (weight.shape[1],))


def rotate_pairs(values, positions, heads):
    features = values.shape[-1]
    head_dim = features // heads
    half = head_dim // 2
    freqs = jnp.power(10000.0, -jnp.arange(half, dtype=jnp.float32) / half)
    angle = (positions % ROT_PERIOD).astype(jnp.float32)[:, None] * freqs[None, :]
    cosine = jnp.cos(angle)[:, None, :]
    sine = jnp.sin(angle)[:, None, :]
    shaped = values.reshape(values.shape[:-1] + (heads, head_dim))
    first = shaped[..., :half]
    second = shaped[..., half:]
    turned = jnp.concatenate(
        [first * cosine - second * sine, first * sine + second * cosine], axis=-1
    )
    return turned.reshape(values.shape)


def body(
    state_tokens,
    gain_time,
    query_time,
    key_time,
    value_time,
    output_time,
    gain_space,
    query_space,
    key_space,
    value_space,
    output_space,
    neighbours,
):
    frames_here, tokens_here, features = state_tokens.shape
    head_dim = features // HEADS
    score_scale = 1.0 / jnp.sqrt(jnp.float32(head_dim))
    frame_count = lax.axis_size("frame")
    normed = rms_scale(state_tokens, gain_time)
    split_rows = normed.reshape(frames_here, frame_count, tokens_here // frame_count, features)
    shard_rows = lax.all_to_all(split_rows, "frame", split_axis=1, concat_axis=0, tiled=True)
    frames, unused_one, item_count, unused_width = shard_rows.shape
    flat_rows = shard_rows.reshape(frames, item_count, features)
    t_query = (
        project_rows(flat_rows, query_time)
        .astype(jnp.bfloat16)
        .reshape(frames, item_count, HEADS, head_dim)
    )
    t_key = (
        project_rows(flat_rows, key_time)
        .astype(jnp.bfloat16)
        .reshape(frames, item_count, HEADS, head_dim)
    )
    t_value = (
        project_rows(flat_rows, value_time)
        .astype(jnp.bfloat16)
        .reshape(frames, item_count, HEADS, head_dim)
    )
    scores = (
        jnp.einsum("fghd,eghd->ghfe", t_query, t_key, preferred_element_type=jnp.float32)
        * score_scale
    )
    weights = jax.nn.softmax(scores, axis=-1).astype(jnp.bfloat16)
    result = jnp.einsum("ghfe,eghd->fghd", weights, t_value, preferred_element_type=jnp.float32)
    gathered = result.astype(jnp.bfloat16).reshape(frames, 1, item_count, features)
    returned = lax.all_to_all(gathered, "frame", split_axis=0, concat_axis=1, tiled=True)
    returned = returned.reshape(frames_here, tokens_here, features)
    middle = (state_tokens.astype(jnp.float32) + project_rows(returned, output_time)).astype(
        jnp.bfloat16
    )
    normed_space = rms_scale(middle, gain_space)
    tile_place = lax.axis_index("tile")
    tile_count = lax.axis_size("tile")
    token_total = tile_count * tokens_here
    own_positions = tile_place * tokens_here + jnp.arange(tokens_here, dtype=jnp.int32)
    space_query = rotate_pairs(
        project_rows(normed_space, query_space), own_positions, HEADS
    ).astype(jnp.bfloat16)
    wide_rows = padded(normed_space, (("tile", 1),), tokens_here)
    wide_positions = (
        (tile_place - 1) * tokens_here + jnp.arange(3 * tokens_here, dtype=jnp.int32)
    ) % token_total
    space_key = rotate_pairs(project_rows(wide_rows, key_space), wide_positions, HEADS).astype(
        jnp.bfloat16
    )
    space_value = project_rows(wide_rows, value_space).astype(jnp.bfloat16)
    local_blocks = tokens_here // BLOCK
    block_total = local_blocks * tile_count
    group_count = local_blocks // 4
    valid_slot = neighbours >= 0
    local_ids = (neighbours - (tile_place - 1) * local_blocks) % block_total
    local_ids = jnp.where(valid_slot, local_ids, 0)
    key_blocks = space_key.reshape(frames_here, 3 * local_blocks, BLOCK, features)
    value_blocks = space_value.reshape(frames_here, 3 * local_blocks, BLOCK, features)
    query_blocks = space_query.reshape(frames_here, group_count, 4, BLOCK, features)
    id_groups = local_ids.reshape(group_count, 4, NEIGHBOUR_COUNT)
    slot_groups = valid_slot.reshape(group_count, 4, NEIGHBOUR_COUNT)

    def attend_group(group_index):
        query = query_blocks[:, group_index]
        block_ids = id_groups[group_index]
        gathered_keys = key_blocks[:, block_ids].reshape(
            frames_here, 4, NEIGHBOUR_COUNT * BLOCK, features
        )
        gathered_values = value_blocks[:, block_ids].reshape(
            frames_here, 4, NEIGHBOUR_COUNT * BLOCK, features
        )
        key_mask = jnp.repeat(slot_groups[group_index], BLOCK, axis=1)
        head_outs = []
        for head_index in range(HEADS):
            lower = head_index * head_dim
            upper = lower + head_dim
            scores = (
                jnp.einsum(
                    "fbqd,fbkd->fbqk",
                    query[..., lower:upper],
                    gathered_keys[..., lower:upper],
                    preferred_element_type=jnp.float32,
                )
                * score_scale
            )
            scores = jnp.where(key_mask[None, :, None, :], scores, -1e30)
            weights = jax.nn.softmax(scores, axis=-1).astype(jnp.bfloat16)
            result = jnp.einsum(
                "fbqk,fbkd->fbqd",
                weights,
                gathered_values[..., lower:upper],
                preferred_element_type=jnp.float32,
            )
            head_outs.append(result.astype(jnp.bfloat16))
        return jnp.concatenate(head_outs, axis=-1)

    attended = lax.map(attend_group, jnp.arange(group_count, dtype=jnp.int32))
    attended = jnp.moveaxis(attended, 0, 1).reshape(frames_here, tokens_here, features)
    return (middle.astype(jnp.float32) + project_rows(attended, output_space)).astype(jnp.bfloat16)


def solution(mesh):
    return jax.shard_map(
        body,
        mesh=mesh,
        in_specs=(
            P("frame", "tile", None),
            P(),
            P(),
            P(),
            P(),
            P(),
            P(),
            P(),
            P(),
            P(),
            P(),
            P("tile", None),
        ),
        out_specs=P("frame", "tile", None),
        check_vma=False,
    )
```

profile of v0, /device:TPU:63, one launch (start us, length us, event | category | flops | bytes accessed | tf_op | source)
XLA Modules:
  0.0 278.0 jit_solution(10069312233926066814)
XLA Ops:
  2.6 51.6 %all_to_all.8 = bf16[1,16,64,256]{3,2,0,1:T(8,128)(2,1)S(1)} all-to-all(bf16[1,16,64,256]{3,2,0,1:T(8,128)(2,1)S(1)} %bitcast.489), channel_id=1, replica_groups=mesh['frame'=16,'tile'=32] {'frame'}, dimensions={1} | all-to-all | bytes 1048576 | tf_op jit(solution)/shard_map/all_to_all | solution.py:77
  55.0 3.9 %copy.100 = bf16[16,64,8,32]{3,0,2,1:T(8,128)(2,1)} copy(bf16[16,64,8,32]{1,3,2,0:T(8,128)(2,1)S(1)} %bitcast.485) | data formatting | bytes 1048576 | tf_op jit(solution)/shard_map/reshape | solution.py:83
  59.7 3.9 %copy.101 = bf16[16,64,8,32]{3,0,2,1:T(8,128)(2,1)} copy(bf16[16,64,8,32]{1,3,2,0:T(8,128)(2,1)S(1)} %bitcast.486) | data formatting | bytes 1048576 | tf_op jit(solution)/shard_map/reshape | solution.py:88
  64.4 3.9 %copy.102 = bf16[16,64,8,32]{3,0,2,1:T(8,128)(2,1)} copy(bf16[16,64,8,32]{1,3,2,0:T(8,128)(2,1)S(1)} %bitcast.487) | data formatting | bytes 1048576 | tf_op jit(solution)/shard_map/reshape | solution.py:93
  68.4 5.6 %fusion.138 = (f32[64,8,16]{2,1,0:T(8,128)S(1)}, f32[64,8,16,16]{2,3,1,0:T(8,128)}) fusion(bf16[16,64,8,32]{3,0,2,1:T(8,128)(2,1)S(1)} %copy-done.4, bf16[16,64,8,32]{3,0,2,1:T(8,128)(2,1)} %copy.101), kind=kOutput, calls=%fused_computation.230 | convolution fusion | flops 8781839 | bytes 1605632 | tf_op jit(solution)/shard_map/sub | solution.py:99
  74.0 3.7 %convert_bitcast_fusion = bf16[16,64,8,32]{3,0,2,1:T(8,128)(2,1)S(1)} fusion(bf16[16,64,8,32]{3,0,2,1:T(8,128)(2,1)} %copy.102, f32[64,8,16,16]{2,3,1,0:T(8,128)} %get-tuple-element.121, f32[64,8,16]{2,1,0:T(8,128)S(1)} %get-tuple-element.120), kind=kOutput, calls=%fused_computation.146 | convolution fusion | flops 8912896 | bytes 1605632 | tf_op jit(solution)/shard_map/ghfe,eghd->fghd/dot_general | solution.py:100
  77.7 2.4 copy.104
  81.3 5.6 %all-to-all-start.1 = ((bf16[16,1,64,256]{3,2,1,0:T(8,128)(2,1)}), bf16[16,1,64,256]{3,2,1,0:T(8,128)(2,1)S(1)}, u32[]{:S(2)}, u32[]{:S(2)}) async-start(bf16[16,1,64,256]{3,2,1,0:T(8,128)(2,1)} %copy.105), calls=%async_computation.1 | async-start | bytes 1048576 | tf_op jit(solution)/shard_map/all_to_all | solution.py:102
  88.8 20.5 %all-to-all-done.1 = bf16[16,1,64,256]{3,2,1,0:T(8,128)(2,1)S(1)} async-done(((bf16[16,1,64,256]{3,2,1,0:T(8,128)(2,1)}), bf16[16,1,64,256]{3,2,1,0:T(8,128)(2,1)S(1)}, u32[]{:S(2)}, u32[]{:S(2)}) %all-to-all-start.1) | async-done | bytes 524320 | tf_op jit(solution)/shard_map/all_to_all | solution.py:102
  110.0 11.6 %collective-permute-start = (bf16[1,1024,256]{2,1,0:T(8,128)(2,1)S(1)}, bf16[1,1024,256]{2,1,0:T(8,128)(2,1)S(1)}, u32[]{:S(2)}, u32[]{:S(2)}) collective-permute-start(bf16[1,1024,256]{2,1,0:T(8,128)(2,1)S(1)} %fusion.104), channel_id=1, source_target_pairs={{0,1},{1,2},{2,3},{3,4},{4,5},{5,6},{6,7},{7,8},{8,9},{9,10},{10,1... | collective-permute-start | bytes 1572872 | tf_op jit(solution)/shard_map/ppermute | solution.py:22
  125.2 2.5 collective-permute-done
  127.6 5.9 %collective-permute-done.1 = bf16[1,1024,256]{2,1,0:T(8,128)(2,1)S(1)} collective-permute-done((bf16[1,1024,256]{2,1,0:T(8,128)(2,1)S(1)}, bf16[1,1024,256]{2,1,0:T(8,128)(2,1)S(1)}, u32[]{:S(2)}, u32[]{:S(2)}) %collective-permute-start.1) | collective-permute-done | bytes 524320 | tf_op jit(solution)/shard_map/ppermute | solution.py:23
  138.8 136.8 %while.10 = (s32[]{:T(128)}, bf16[2,1,4,128,256]{4,3,2,0,1:T(8,128)(2,1)}, s32[2]{0:T(128)}, pred[2,4,9]{2,1,0:T(4,128)(4,1)}, bf16[1,2,4,128,256]{3,2,1,4,0:T(4...) while((s32[]{:T(128)}, ...), condition=%wide.region_21.22_spmd, body=%wide.region_4.21_spmd.sunk | while | flops 632432768 | bytes 70868280 | solution.py:169
  142.2 2.3 gather_fusion.1
  146.3 4.2 %fusion.167 = (f32[4,128]{1,0:T(4,128)}, f32[4,128,1152]{2,1,0:T(8,128)}) fusion(bf16[1,4,1152,256]{3,2,1,0:T(8,128)(2,1)} %bitcast.458, pred[4,1152]{1,0:T(4,128)(4,1)S(1)} %bitcast.494, bf16[1,4,128,256]{2,3,1,0:T(8,128)(2,1)S(1)} %bitcast.474), kind=kOutput, calls=%fused_computation.222.clone.1 | convolution fusion | flops 40109184 | bytes 3578368 | tf_op jit(solution)/shard_map/while/body/eval_jaxpr/sub | solution.py:159
  152.8 2.6 fusion.168
  155.5 3.9 %fusion.169 = (f32[4,128]{1,0:T(4,128)S(1)}, f32[4,128,1152]{2,1,0:T(8,128)}) fusion(bf16[1,4,1152,256]{3,2,1,0:T(8,128)(2,1)} %bitcast.459, pred[4,1152]{1,0:T(4,128)(4,1)S(1)} %bitcast.495, bf16[1,4,128,256]{2,3,1,0:T(8,128)(2,1)} %bitcast.475), kind=kOutput, calls=%fused_computation.223.clone.1 | convolution fusion | flops 40109184 | bytes 3578368 | tf_op jit(solution)/shard_map/while/body/eval_jaxpr/sub | solution.py:159
  159.4 3.3 %fusion.170 = bf16[1,4,128,256]{2,3,1,0:T(8,128)(2,1)S(1)} fusion(bf16[1,4,128,256]{2,3,1,0:T(8,128)(2,1)S(1)} %fusion.168, bf16[1,4,1152,256]{3,2,1,0:T(8,128)(2,1)} %bitcast.467, f32[4,128,1152]{2,1,0:T(8,128)} %get-tuple-element.191, f32[4,128]{1,0:T(4,128)S(1)} %get-tuple-element.192), kind=kOutput, calls=%fused_computation.95.clone.1 | convolution fusion | flops 38944768 | bytes 3573760 | tf_op jit(solution)/shard_map/while/body/eval_jaxpr/fbqk,fbkd->fbqd/dot_general | solution.py:160
  162.6 3.9 %fusion.171 = (f32[4,128]{1,0:T(4,128)S(1)}, f32[4,128,1152]{2,1,0:T(8,128)}) fusion(bf16[1,4,1152,256]{3,2,1,0:T(8,128)(2,1)} %bitcast.460, pred[4,1152]{1,0:T(4,128)(4,1)S(1)} %bitcast.496, bf16[1,4,128,256]{2,3,1,0:T(8,128)(2,1)} %bitcast.476), kind=kOutput, calls=%fused_computation.224.clone.1 | convolution fusion | flops 40109184 | bytes 3578368 | tf_op jit(solution)/shard_map/while/body/eval_jaxpr/sub | solution.py:159
  166.5 3.3 %fusion.172 = bf16[1,4,128,256]{2,3,1,0:T(8,128)(2,1)S(1)} fusion(bf16[1,4,128,256]{2,3,1,0:T(8,128)(2,1)S(1)} %fusion.170, bf16[1,4,1152,256]{3,2,1,0:T(8,128)(2,1)} %bitcast.468, f32[4,128,1152]{2,1,0:T(8,128)} %get-tuple-element.193, f32[4,128]{1,0:T(4,128)S(1)} %get-tuple-element.194), kind=kOutput, calls=%fused_computation.93.clone.1 | convolution fusion | flops 38944768 | bytes 3573760 | tf_op jit(solution)/shard_map/while/body/eval_jaxpr/fbqk,fbkd->fbqd/dot_general | solution.py:160
  169.8 3.9 %fusion.173 = (f32[4,128]{1,0:T(4,128)S(1)}, f32[4,128,1152]{2,1,0:T(8,128)}) fusion(bf16[1,4,1152,256]{3,2,1,0:T(8,128)(2,1)} %bitcast.461, pred[4,1152]{1,0:T(4,128)(4,1)S(1)} %bitcast.497, bf16[1,4,128,256]{2,3,1,0:T(8,128)(2,1)} %bitcast.477), kind=kOutput, calls=%fused_computation.225.clone.1 | convolution fusion | flops 40109184 | bytes 3578368 | tf_op jit(solution)/shard_map/while/body/eval_jaxpr/sub | solution.py:159
  173.7 3.3 %fusion.174 = bf16[1,4,128,256]{2,3,1,0:T(8,128)(2,1)S(1)} fusion(bf16[1,4,128,256]{2,3,1,0:T(8,128)(2,1)S(1)} %fusion.172, bf16[1,4,1152,256]{3,2,1,0:T(8,128)(2,1)} %bitcast.469, f32[4,128,1152]{2,1,0:T(8,128)} %get-tuple-element.195, f32[4,128]{1,0:T(4,128)S(1)} %get-tuple-element.196), kind=kOutput, calls=%fused_computation.91.clone.1 | convolution fusion | flops 38944768 | bytes 3573760 | tf_op jit(solution)/shard_map/while/body/eval_jaxpr/fbqk,fbkd->fbqd/dot_general | solution.py:160
  177.0 3.7 %fusion.175 = (f32[4,128]{1,0:T(4,128)S(1)}, f32[4,128,1152]{2,1,0:T(8,128)}) fusion(bf16[1,4,1152,256]{3,2,1,0:T(8,128)(2,1)} %bitcast.462, pred[4,1152]{1,0:T(4,128)(4,1)S(1)} %bitcast.498, bf16[1,4,128,256]{2,3,1,0:T(8,128)(2,1)} %bitcast.478), kind=kOutput, calls=%fused_computation.226.clone.1 | convolution fusion | flops 40109184 | bytes 3578368 | tf_op jit(solution)/shard_map/while/body/eval_jaxpr/sub | solution.py:159
  180.6 2.7 fusion.176
  183.3 3.9 %fusion.177 = (f32[4,128]{1,0:T(4,128)S(1)}, f32[4,128,1152]{2,1,0:T(8,128)}) fusion(bf16[1,4,1152,256]{3,2,1,0:T(8,128)(2,1)} %bitcast.463, pred[4,1152]{1,0:T(4,128)(4,1)S(1)} %bitcast.499, bf16[1,4,128,256]{2,3,1,0:T(8,128)(2,1)} %bitcast.479), kind=kOutput, calls=%fused_computation.227.clone.1 | convolution fusion | flops 40109184 | bytes 3578368 | tf_op jit(solution)/shard_map/while/body/eval_jaxpr/sub | solution.py:159
  187.2 3.3 %fusion.178 = bf16[1,4,128,256]{2,3,1,0:T(8,128)(2,1)S(1)} fusion(bf16[1,4,128,256]{2,3,1,0:T(8,128)(2,1)S(1)} %fusion.176, bf16[1,4,1152,256]{3,2,1,0:T(8,128)(2,1)} %bitcast.471, f32[4,128,1152]{2,1,0:T(8,128)} %get-tuple-element.199, f32[4,128]{1,0:T(4,128)S(1)} %get-tuple-element.200), kind=kOutput, calls=%fused_computation.87.clone.1 | convolution fusion | flops 38944768 | bytes 3573760 | tf_op jit(solution)/shard_map/while/body/eval_jaxpr/fbqk,fbkd->fbqd/dot_general | solution.py:160
  190.5 3.9 %fusion.179 = (f32[4,128]{1,0:T(4,128)S(1)}, f32[4,128,1152]{2,1,0:T(8,128)}) fusion(bf16[1,4,1152,256]{3,2,1,0:T(8,128)(2,1)} %bitcast.464, pred[4,1152]{1,0:T(4,128)(4,1)S(1)} %bitcast.500, bf16[1,4,128,256]{2,3,1,0:T(8,128)(2,1)} %bitcast.480), kind=kOutput, calls=%fused_computation.228.clone.1 | convolution fusion | flops 40109184 | bytes 3578368 | tf_op jit(solution)/shard_map/while/body/eval_jaxpr/sub | solution.py:159
  194.3 3.3 %fusion.180 = bf16[1,4,128,256]{2,3,1,0:T(8,128)(2,1)S(1)} fusion(bf16[1,4,128,256]{2,3,1,0:T(8,128)(2,1)S(1)} %fusion.178, bf16[1,4,1152,256]{3,2,1,0:T(8,128)(2,1)} %bitcast.472, f32[4,128,1152]{2,1,0:T(8,128)} %get-tuple-element.201, f32[4,128]{1,0:T(4,128)S(1)} %get-tuple-element.202), kind=kOutput, calls=%fused_computation.85.clone.1 | convolution fusion | flops 38944768 | bytes 3573760 | tf_op jit(solution)/shard_map/while/body/eval_jaxpr/fbqk,fbkd->fbqd/dot_general | solution.py:160
  197.6 3.9 %fusion.181 = (f32[4,128]{1,0:T(4,128)S(1)}, f32[4,128,1152]{2,1,0:T(8,128)}) fusion(bf16[1,4,1152,256]{3,2,1,0:T(8,128)(2,1)} %bitcast.465, pred[4,1152]{1,0:T(4,128)(4,1)S(1)} %bitcast.501, bf16[1,4,128,256]{2,3,1,0:T(8,128)(2,1)} %bitcast.481), kind=kOutput, calls=%fused_computation.229.clone.1 | convolution fusion | flops 40109184 | bytes 3578368 | tf_op jit(solution)/shard_map/while/body/eval_jaxpr/sub | solution.py:159
  201.5 3.3 %fusion.182 = bf16[1,4,128,256]{2,3,1,0:T(8,128)(2,1)S(1)} fusion(bf16[1,4,128,256]{2,3,1,0:T(8,128)(2,1)S(1)} %fusion.180, bf16[1,4,1152,256]{3,2,1,0:T(8,128)(2,1)} %bitcast.473, f32[4,128,1152]{2,1,0:T(8,128)} %get-tuple-element.203, f32[4,128]{1,0:T(4,128)S(1)} %get-tuple-element.204), kind=kOutput, calls=%fused_computation.83.clone.1 | convolution fusion | flops 38944768 | bytes 3573760 | tf_op jit(solution)/shard_map/while/body/eval_jaxpr/fbqk,fbkd->fbqd/dot_general | solution.py:160
  210.6 2.3 gather_fusion.1
  214.7 4.2 %fusion.167 = (f32[4,128]{1,0:T(4,128)}, f32[4,128,1152]{2,1,0:T(8,128)}) fusion(bf16[1,4,1152,256]{3,2,1,0:T(8,128)(2,1)} %bitcast.458, pred[4,1152]{1,0:T(4,128)(4,1)S(1)} %bitcast.494, bf16[1,4,128,256]{2,3,1,0:T(8,128)(2,1)S(1)} %bitcast.474), kind=kOutput, calls=%fused_computation.222.clone.1 | convolution fusion | flops 40109184 | bytes 3578368 | tf_op jit(solution)/shard_map/while/body/eval_jaxpr/sub | solution.py:159
  221.2 2.7 fusion.168
  223.9 3.9 %fusion.169 = (f32[4,128]{1,0:T(4,128)S(1)}, f32[4,128,1152]{2,1,0:T(8,128)}) fusion(bf16[1,4,1152,256]{3,2,1,0:T(8,128)(2,1)} %bitcast.459, pred[4,1152]{1,0:T(4,128)(4,1)S(1)} %bitcast.495, bf16[1,4,128,256]{2,3,1,0:T(8,128)(2,1)} %bitcast.475), kind=kOutput, calls=%fused_computation.223.clone.1 | convolution fusion | flops 40109184 | bytes 3578368 | tf_op jit(solution)/shard_map/while/body/eval_jaxpr/sub | solution.py:159
  227.8 3.3 %fusion.170 = bf16[1,4,128,256]{2,3,1,0:T(8,128)(2,1)S(1)} fusion(bf16[1,4,128,256]{2,3,1,0:T(8,128)(2,1)S(1)} %fusion.168, bf16[1,4,1152,256]{3,2,1,0:T(8,128)(2,1)} %bitcast.467, f32[4,128,1152]{2,1,0:T(8,128)} %get-tuple-element.191, f32[4,128]{1,0:T(4,128)S(1)} %get-tuple-element.192), kind=kOutput, calls=%fused_computation.95.clone.1 | convolution fusion | flops 38944768 | bytes 3573760 | tf_op jit(solution)/shard_map/while/body/eval_jaxpr/fbqk,fbkd->fbqd/dot_general | solution.py:160
  231.0 3.9 %fusion.171 = (f32[4,128]{1,0:T(4,128)S(1)}, f32[4,128,1152]{2,1,0:T(8,128)}) fusion(bf16[1,4,1152,256]{3,2,1,0:T(8,128)(2,1)} %bitcast.460, pred[4,1152]{1,0:T(4,128)(4,1)S(1)} %bitcast.496, bf16[1,4,128,256]{2,3,1,0:T(8,128)(2,1)} %bitcast.476), kind=kOutput, calls=%fused_computation.224.clone.1 | convolution fusion | flops 40109184 | bytes 3578368 | tf_op jit(solution)/shard_map/while/body/eval_jaxpr/sub | solution.py:159
  234.9 3.3 %fusion.172 = bf16[1,4,128,256]{2,3,1,0:T(8,128)(2,1)S(1)} fusion(bf16[1,4,128,256]{2,3,1,0:T(8,128)(2,1)S(1)} %fusion.170, bf16[1,4,1152,256]{3,2,1,0:T(8,128)(2,1)} %bitcast.468, f32[4,128,1152]{2,1,0:T(8,128)} %get-tuple-element.193, f32[4,128]{1,0:T(4,128)S(1)} %get-tuple-element.194), kind=kOutput, calls=%fused_computation.93.clone.1 | convolution fusion | flops 38944768 | bytes 3573760 | tf_op jit(solution)/shard_map/while/body/eval_jaxpr/fbqk,fbkd->fbqd/dot_general | solution.py:160
  238.2 3.9 %fusion.173 = (f32[4,128]{1,0:T(4,128)S(1)}, f32[4,128,1152]{2,1,0:T(8,128)}) fusion(bf16[1,4,1152,256]{3,2,1,0:T(8,128)(2,1)} %bitcast.461, pred[4,1152]{1,0:T(4,128)(4,1)S(1)} %bitcast.497, bf16[1,4,128,256]{2,3,1,0:T(8,128)(2,1)} %bitcast.477), kind=kOutput, calls=%fused_computation.225.clone.1 | convolution fusion | flops 40109184 | bytes 3578368 | tf_op jit(solution)/shard_map/while/body/eval_jaxpr/sub | solution.py:159
  242.1 3.3 %fusion.174 = bf16[1,4,128,256]{2,3,1,0:T(8,128)(2,1)S(1)} fusion(bf16[1,4,128,256]{2,3,1,0:T(8,128)(2,1)S(1)} %fusion.172, bf16[1,4,1152,256]{3,2,1,0:T(8,128)(2,1)} %bitcast.469, f32[4,128,1152]{2,1,0:T(8,128)} %get-tuple-element.195, f32[4,128]{1,0:T(4,128)S(1)} %get-tuple-element.196), kind=kOutput, calls=%fused_computation.91.clone.1 | convolution fusion | flops 38944768 | bytes 3573760 | tf_op jit(solution)/shard_map/while/body/eval_jaxpr/fbqk,fbkd->fbqd/dot_general | solution.py:160
  245.3 3.7 %fusion.175 = (f32[4,128]{1,0:T(4,128)S(1)}, f32[4,128,1152]{2,1,0:T(8,128)}) fusion(bf16[1,4,1152,256]{3,2,1,0:T(8,128)(2,1)} %bitcast.462, pred[4,1152]{1,0:T(4,128)(4,1)S(1)} %bitcast.498, bf16[1,4,128,256]{2,3,1,0:T(8,128)(2,1)} %bitcast.478), kind=kOutput, calls=%fused_computation.226.clone.1 | convolution fusion | flops 40109184 | bytes 3578368 | tf_op jit(solution)/shard_map/while/body/eval_jaxpr/sub | solution.py:159
  249.0 2.7 fusion.176
  251.7 3.9 %fusion.177 = (f32[4,128]{1,0:T(4,128)S(1)}, f32[4,128,1152]{2,1,0:T(8,128)}) fusion(bf16[1,4,1152,256]{3,2,1,0:T(8,128)(2,1)} %bitcast.463, pred[4,1152]{1,0:T(4,128)(4,1)S(1)} %bitcast.499, bf16[1,4,128,256]{2,3,1,0:T(8,128)(2,1)} %bitcast.479), kind=kOutput, calls=%fused_computation.227.clone.1 | convolution fusion | flops 40109184 | bytes 3578368 | tf_op jit(solution)/shard_map/while/body/eval_jaxpr/sub | solution.py:159
  255.6 3.3 %fusion.178 = bf16[1,4,128,256]{2,3,1,0:T(8,128)(2,1)S(1)} fusion(bf16[1,4,128,256]{2,3,1,0:T(8,128)(2,1)S(1)} %fusion.176, bf16[1,4,1152,256]{3,2,1,0:T(8,128)(2,1)} %bitcast.471, f32[4,128,1152]{2,1,0:T(8,128)} %get-tuple-element.199, f32[4,128]{1,0:T(4,128)S(1)} %get-tuple-element.200), kind=kOutput, calls=%fused_computation.87.clone.1 | convolution fusion | flops 38944768 | bytes 3573760 | tf_op jit(solution)/shard_map/while/body/eval_jaxpr/fbqk,fbkd->fbqd/dot_general | solution.py:160
  258.8 3.9 %fusion.179 = (f32[4,128]{1,0:T(4,128)S(1)}, f32[4,128,1152]{2,1,0:T(8,128)}) fusion(bf16[1,4,1152,256]{3,2,1,0:T(8,128)(2,1)} %bitcast.464, pred[4,1152]{1,0:T(4,128)(4,1)S(1)} %bitcast.500, bf16[1,4,128,256]{2,3,1,0:T(8,128)(2,1)} %bitcast.480), kind=kOutput, calls=%fused_computation.228.clone.1 | convolution fusion | flops 40109184 | bytes 3578368 | tf_op jit(solution)/shard_map/while/body/eval_jaxpr/sub | solution.py:159
  262.7 3.3 %fusion.180 = bf16[1,4,128,256]{2,3,1,0:T(8,128)(2,1)S(1)} fusion(bf16[1,4,128,256]{2,3,1,0:T(8,128)(2,1)S(1)} %fusion.178, bf16[1,4,1152,256]{3,2,1,0:T(8,128)(2,1)} %bitcast.472, f32[4,128,1152]{2,1,0:T(8,128)} %get-tuple-element.201, f32[4,128]{1,0:T(4,128)S(1)} %get-tuple-element.202), kind=kOutput, calls=%fused_computation.85.clone.1 | convolution fusion | flops 38944768 | bytes 3573760 | tf_op jit(solution)/shard_map/while/body/eval_jaxpr/fbqk,fbkd->fbqd/dot_general | solution.py:160
  266.0 3.9 %fusion.181 = (f32[4,128]{1,0:T(4,128)S(1)}, f32[4,128,1152]{2,1,0:T(8,128)}) fusion(bf16[1,4,1152,256]{3,2,1,0:T(8,128)(2,1)} %bitcast.465, pred[4,1152]{1,0:T(4,128)(4,1)S(1)} %bitcast.501, bf16[1,4,128,256]{2,3,1,0:T(8,128)(2,1)} %bitcast.481), kind=kOutput, calls=%fused_computation.229.clone.1 | convolution fusion | flops 40109184 | bytes 3578368 | tf_op jit(solution)/shard_map/while/body/eval_jaxpr/sub | solution.py:159
  269.9 3.3 %fusion.182 = bf16[1,4,128,256]{2,3,1,0:T(8,128)(2,1)S(1)} fusion(bf16[1,4,128,256]{2,3,1,0:T(8,128)(2,1)S(1)} %fusion.180, bf16[1,4,1152,256]{3,2,1,0:T(8,128)(2,1)} %bitcast.473, f32[4,128,1152]{2,1,0:T(8,128)} %get-tuple-element.203, f32[4,128]{1,0:T(4,128)S(1)} %get-tuple-element.204), kind=kOutput, calls=%fused_computation.83.clone.1 | convolution fusion | flops 38944768 | bytes 3573760 | tf_op jit(solution)/shard_map/while/body/eval_jaxpr/fbqk,fbkd->fbqd/dot_general | solution.py:160
  275.6 2.4 fusion.98
  (97 shorter events, 33.1 us)
Async XLA Ops:
  0.0 136.4 %copy-start = (bf16[256,256]{1,0:T(8,128)(2,1)S(1)}, bf16[256,256]{1,0:T(8,128)(2,1)}, u32[]{:S(2)}) copy-start(bf16[256,256]{1,0:T(8,128)(2,1)} %param.23) | copy-start | bytes 393220
  0.0 54.2 %copy-start.7 = (bf16[256,256]{1,0:T(8,128)(2,1)S(1)}, bf16[256,256]{1,0:T(8,128)(2,1)}, u32[]{:S(2)}) copy-start(bf16[256,256]{1,0:T(8,128)(2,1)} %param.16) | copy-start | bytes 393220
  54.5 4.4 %copy-start.8 = (bf16[256,256]{1,0:T(8,128)(2,1)S(1)}, bf16[256,256]{1,0:T(8,128)(2,1)}, u32[]{:S(2)}) copy-start(bf16[256,256]{1,0:T(8,128)(2,1)} %param.17) | copy-start | bytes 393220
  59.2 4.4 %copy-start.9 = (bf16[256,256]{1,0:T(8,128)(2,1)S(1)}, bf16[256,256]{1,0:T(8,128)(2,1)}, u32[]{:S(2)}) copy-start(bf16[256,256]{1,0:T(8,128)(2,1)} %param.18) | copy-start | bytes 393220
  64.4 3.9 %copy-start.4 = (bf16[16,64,8,32]{3,0,2,1:T(8,128)(2,1)S(1)}, bf16[16,64,8,32]{3,0,2,1:T(8,128)(2,1)}, u32[]{:S(2)}) copy-start(bf16[16,64,8,32]{3,0,2,1:T(8,128)(2,1)} %copy.100) | copy-start | bytes 1572868
  77.7 9.2 %copy-start.10 = (bf16[256,256]{1,0:T(8,128)(2,1)S(1)}, bf16[256,256]{1,0:T(8,128)(2,1)}, u32[]{:S(2)}) copy-start(bf16[256,256]{1,0:T(8,128)(2,1)} %param.22) | copy-start | bytes 393220
  77.7 9.3 %copy-start.11 = (bf16[256,256]{1,0:T(8,128)(2,1)S(1)}, bf16[256,256]{1,0:T(8,128)(2,1)}, u32[]{:S(2)}) copy-start(bf16[256,256]{1,0:T(8,128)(2,1)} %param.21) | copy-start | bytes 393220
  80.1 7.1 %copy-start.12 = (s32[8,9]{1,0:T(8,128)S(1)}, s32[8,9]{1,0:T(8,128)}, u32[]{:S(2)}) copy-start(s32[8,9]{1,0:T(8,128)} %param.25) | copy-start | bytes 868
  80.1 29.2 %copy-start.5 = (bf16[1,1024,256]{2,1,0:T(8,128)(2,1)S(1)}, bf16[1,1024,256]{2,1,0:T(8,128)(2,1)}, u32[]{:S(2)}) copy-start(bf16[1,1024,256]{2,1,0:T(8,128)(2,1)} %param.14) | copy-start | bytes 1572868
  80.1 29.2 %copy-start.16 = (bf16[256,256]{1,0:T(8,128)(2,1)S(1)}, bf16[256,256]{1,0:T(8,128)(2,1)}, u32[]{:S(2)}) copy-start(bf16[256,256]{1,0:T(8,128)(2,1)} %param.19) | copy-start | bytes 393220
  81.3 28.5 %copy-start.13 = (f32[256]{0:T(256)S(1)}, f32[256]{0:T(256)}, u32[]{:S(2)}) copy-start(f32[256]{0:T(256)} %param.20) | copy-start | bytes 3076
  81.3 28.0 %all-to-all-start.1 = ((bf16[16,1,64,256]{3,2,1,0:T(8,128)(2,1)}), bf16[16,1,64,256]{3,2,1,0:T(8,128)(2,1)S(1)}, u32[]{:S(2)}, u32[]{:S(2)}) async-start(bf16[16,1,64,256]{3,2,1,0:T(8,128)(2,1)} %copy.105), calls=%async_computation.1 | async-start | bytes 1048576 | tf_op jit(solution)/shard_map/all_to_all | solution.py:102
  109.7 14.3 %copy-start.6 = (bf16[1,1024,256]{2,1,0:T(8,128)(2,1)}, bf16[1,1024,256]{2,1,0:T(8,128)(2,1)S(1)}, u32[]{:S(2)}) copy-start(bf16[1,1024,256]{2,1,0:T(8,128)(2,1)S(1)} %get-tuple-element.123) | copy-start | bytes 1572868
  110.0 23.6 %copy-start.3 = (bf16[1,1024,256]{2,1,0:T(8,128)(2,1)}, bf16[1,1024,256]{2,1,0:T(8,128)(2,1)S(1)}, u32[]{:S(2)}) copy-start(bf16[1,1024,256]{2,1,0:T(8,128)(2,1)S(1)} %fusion.104) | copy-start | bytes 1572868
  110.0 17.7 %collective-permute-start = (bf16[1,1024,256]{2,1,0:T(8,128)(2,1)S(1)}, bf16[1,1024,256]{2,1,0:T(8,128)(2,1)S(1)}, u32[]{:S(2)}, u32[]{:S(2)}) collective-permute-start(bf16[1,1024,256]{2,1,0:T(8,128)(2,1)S(1)} %fusion.104), channel_id=1, source_target_pairs={{0,1},{1,2},{2,3},{3,4},{4,5},{5,6},{6,7},{7,8},{8,9},{9,10},{10,1... | collective-permute-start | bytes 1572872 | tf_op jit(solution)/shard_map/ppermute | solution.py:22
  121.5 12.0 %collective-permute-start.1 = (bf16[1,1024,256]{2,1,0:T(8,128)(2,1)S(1)}, bf16[1,1024,256]{2,1,0:T(8,128)(2,1)S(1)}, u32[]{:S(2)}, u32[]{:S(2)}) collective-permute-start(bf16[1,1024,256]{2,1,0:T(8,128)(2,1)S(1)} %fusion.104), channel_id=1, source_target_pairs={{1,0},{2,1},{3,2},{4,3},{5,4},{6,5},{7,6},{8,7},{9,8},{10,9},{11,1... | collective-permute-start | bytes 1572872 | tf_op jit(solution)/shard_map/ppermute | solution.py:23
  127.6 6.5 %copy-start.14 = (bf16[1,1024,256]{2,1,0:T(8,128)(2,1)}, bf16[1,1024,256]{2,1,0:T(8,128)(2,1)S(1)}, u32[]{:S(2)}) copy-start(bf16[1,1024,256]{2,1,0:T(8,128)(2,1)S(1)} %collective-permute-done) | copy-start | bytes 1572868
  133.6 0.8 copy-start.15
  145.6 5.0 %copy-start.1 = (bf16[1,1,4,128,256]{3,4,2,1,0:T(8,128)(2,1)}, bf16[1,1,4,128,256]{3,4,2,1,0:T(8,128)(2,1)S(1)}, u32[]{:S(2)}) copy-start(bf16[1,1,4,128,256]{3,4,2,1,0:T(8,128)(2,1)S(1)} %copy.141) | copy-start | bytes 786436 | tf_op jit(solution)/shard_map/while
  204.8 0.7 copy-start.2
  214.0 4.9 %copy-start.1 = (bf16[1,1,4,128,256]{3,4,2,1,0:T(8,128)(2,1)}, bf16[1,1,4,128,256]{3,4,2,1,0:T(8,128)(2,1)S(1)}, u32[]{:S(2)}) copy-start(bf16[1,1,4,128,256]{3,4,2,1,0:T(8,128)(2,1)S(1)} %copy.141) | copy-start | bytes 786436 | tf_op jit(solution)/shard_map/while
  273.1 0.7 copy-start.2
where the time goes:
time: 279 us; the launch traced here: 278 us
  matrix products  128 us (46%)
  blocking collectives  51.6 us (18%)
  local copies, waits for them, and re-layouts  40.6 us (15%)
  waiting for transfers between devices  28.9 us (10%)
  starting transfers between devices  19.1 us (7%)
  other arithmetic  5.15 us (2%)
  loops' own time  4.26 us (2%)
    sub x16, matrix products, attend_group(): weights = jax.nn.softmax(scores, axis=-1).astype(jnp.bfloat16)  62.5 us
    all_to_all x1, blocking collectives, body(): lax.all_to_all(split_rows, 'frame', split_axis=1, concat_axis=0, tiled=True)  51.6 us
    dot_general x16, matrix products, attend_group(): jnp.einsum('fbqk,fbkd->fbqd', weights, gathered_values[..., lower:upper],...  49.7 us
    all_to_all x1, waiting for transfers between devices, body(): lax.all_to_all(gathered, 'frame', split_axis=0, concat_axis=1, tiled=True)  20.5 us
    ppermute x1, starting transfers between devices, padded(): before = lax.ppermute(last, axis, up)  11.6 us
    dot_general x8, matrix products, project_rows(): result = jnp.dot(flat, weight, preferred_element_type=jnp.float32)  6.51 us
    ppermute x1, waiting for transfers between devices, padded(): after = lax.ppermute(initial, axis, down)  5.93 us
    sub x1, matrix products, body(): weights = jax.nn.softmax(scores, axis=-1).astype(jnp.bfloat16)  5.61 us
  transfers between devices with their start and end apart: 3, of which 3 were waited for; matrix products, arithmetic and copies ran while one was open for 1% of the time, Pallas kernels for 0%

commit v1 on v0

v1 whole, which is shorter than its diff:
```python
import functools
import math

import jax
import jax.numpy as jnp
import numpy as np
from jax import lax
from jax.experimental import pallas as pl
from jax.experimental.pallas import tpu as pltpu
from jax.sharding import PartitionSpec as P

HEADS = 8
BLOCK = 128
NEIGHBOUR_COUNT = 9
EPS = 1e-05
ROT_PERIOD = 1024
NEG = -1e30
F32 = jnp.float32
BF16 = jnp.bfloat16
MESH = pl.DeviceIdType.MESH


def nt(a, b):
    return lax.dot_general(a, b, (((1,), (1,)), ((), ())), preferred_element_type=F32)


def nn(a, b):
    return lax.dot_general(a, b, (((1,), (0,)), ((), ())), preferred_element_type=F32)


def rms(values, gain):
    square_mean = jnp.mean(values * values, axis=-1, keepdims=True)
    return values * lax.rsqrt(square_mean + EPS) * gain


def head_pair(rows, pair, head_dim):
    lane_head = lax.broadcasted_iota(jnp.int32, rows.shape, 1) // head_dim
    zero = jnp.zeros_like(rows)
    return jnp.concatenate(
        [jnp.where(lane_head == 2 * pair + k, rows, zero) for k in range(2)], axis=0
    )


def pair_result(total, head_dim, count):
    inverse = 1.0 / total[2 * head_dim : 2 * head_dim + 1, :]
    scaled = total[: 2 * head_dim, :] * inverse
    return jnp.concatenate(
        [scaled[:head_dim, :count], scaled[head_dim:, count:]], axis=0
    )


def time_kernel(x_ref, gain_ref, wq_ref, wk_ref, wv_ref, out_ref, norm_ref, att_ref):
    frames, tokens, width = x_ref.shape
    head_dim = width // HEADS
    scale = math.log2(math.e) / math.sqrt(head_dim)
    step = BLOCK // frames
    gain = gain_ref[...]

    def norm_frame(f, carry):
        norm_ref[f] = rms(x_ref[f].astype(F32), gain)
        return carry

    lax.fori_loop(0, frames, norm_frame, 0)
    wv_t = wv_ref[...].astype(F32).T.astype(BF16)
    row = lax.broadcasted_iota(jnp.int32, (BLOCK, 2 * BLOCK), 0)
    column = lax.broadcasted_iota(jnp.int32, (BLOCK, 2 * BLOCK), 1)
    same = (row % step) == (column % step)
    ones = jnp.ones((16, BLOCK), BF16)

    def chunk(i, carry):
        at = pl.ds(pl.multiple_of(i * step, step), step)
        rows = norm_ref[:, at, :].reshape(BLOCK, width).astype(BF16)
        query = (nn(rows, wq_ref[...]) * scale).astype(BF16)
        key = nn(rows, wk_ref[...]).astype(BF16)
        value_t = nt(wv_t, rows).astype(BF16)
        parts = []
        for pair in range(HEADS // 2):
            scores = nt(key, head_pair(query, pair, head_dim))
            scores = jnp.where(same, scores, NEG)
            top = jnp.max(scores, axis=0, keepdims=True)
            weights = jnp.exp2(scores - top).astype(BF16)
            low = 2 * pair * head_dim
            held = jnp.concatenate([value_t[low : low + 2 * head_dim], ones], axis=0)
            parts.append(pair_result(nn(held, weights), head_dim, BLOCK))
        att_ref[:, at, :] = jnp.concatenate(parts, axis=0).T.reshape(frames, step, width)
        return carry

    lax.fori_loop(0, tokens // step, chunk, 0)

    def round_frame(f, carry):
        out_ref[f] = att_ref[f].astype(BF16)
        return carry

    lax.fori_loop(0, frames, round_frame, 0)


def time_attend(rows, gain, wq, wk, wv):
    frames, tokens, width = rows.shape
    vmem = pl.BlockSpec(memory_space=pltpu.VMEM)
    return pl.pallas_call(
        time_kernel,
        out_shape=jax.ShapeDtypeStruct(rows.shape, BF16),
        in_specs=[vmem] * 5,
        out_specs=vmem,
        scratch_shapes=[
            pltpu.VMEM(rows.shape, F32),
            pltpu.VMEM(rows.shape, F32),
        ],
        compiler_params=pltpu.CompilerParams(vmem_limit_bytes=32 << 20),
    )(rows, gain.reshape(1, width), wq, wk, wv)


def swapped(weight):
    wide = weight.astype(F32)
    width = wide.shape[1]
    half = width // HEADS // 2
    lane = lax.broadcasted_iota(jnp.int32, wide.shape, 1)
    ahead = pltpu.roll(wide, width - half, 1)
    behind = pltpu.roll(wide, half, 1)
    return jnp.where(lane % (2 * half) < half, -ahead, behind).astype(BF16)


def space_kernel(
    nbr_ref,
    state_ref,
    ret_ref,
    wt_ref,
    gain_ref,
    wq_ref,
    wk_ref,
    wv_ref,
    wo_ref,
    cos_ref,
    sin_ref,
    out_ref,
    norm_ref,
    mid_ref,
    q_ref,
    k_ref,
    v_ref,
    wqs_ref,
    wks_ref,
    wvt_ref,
    kc_ref,
    s_ref,
    att_ref,
    send_l,
    recv_l,
    send_r,
    recv_r,
):
    blocks = mid_ref.shape[0]
    width = state_ref.shape[-1]
    head_dim = width // HEADS
    scale = math.log2(math.e) / math.sqrt(head_dim)
    tile = lax.axis_index("tile")
    tiles = lax.axis_size("tile")
    left = lax.rem(tile + tiles - 1, tiles)
    right = lax.rem(tile + 1, tiles)
    barrier = pltpu.get_barrier_semaphore()
    for peer in (left, right):
        pl.semaphore_signal(barrier, inc=1, device_id={"tile": peer}, device_id_type=MESH)

    def to_left(j):
        return pltpu.make_async_remote_copy(
            src_ref=norm_ref.at[blocks + j],
            dst_ref=norm_ref.at[2 * blocks + j],
            send_sem=send_l.at[j],
            recv_sem=recv_l.at[j],
            device_id={"tile": left},
            device_id_type=MESH,
        )

    def to_right(j):
        return pltpu.make_async_remote_copy(
            src_ref=norm_ref.at[blocks + j],
            dst_ref=norm_ref.at[j],
            send_sem=send_r.at[j],
            recv_sem=recv_r.at[j],
            device_id={"tile": right},
            device_id_type=MESH,
        )

    gain = gain_ref[...]

    def middle(j, carry):
        at = pl.ds(pl.multiple_of(j * BLOCK, BLOCK), BLOCK)
        mid = (state_ref[at, :].astype(F32) + nn(ret_ref[at, :], wt_ref[...])).astype(BF16)
        mid_ref[j] = mid
        norm_ref[blocks + j] = rms(mid.astype(F32), gain).astype(BF16)
        return carry

    lax.fori_loop(0, blocks, middle, 0)
    pl.semaphore_wait(barrier, 2)

    def send(j, carry):
        to_left(j).start()
        to_right(blocks - 1 - j).start()
        return carry

    lax.fori_loop(0, blocks, send, 0)

    wqs_ref[...] = swapped(wq_ref[...])
    wks_ref[...] = swapped(wk_ref[...])
    wvt_ref[...] = wv_ref[...].astype(F32).T.astype(BF16)

    def turn(rows, weight_ref, swap_ref, j):
        at = pl.ds(pl.multiple_of(j * BLOCK, BLOCK), BLOCK)
        cosine = jnp.concatenate([cos_ref[at, :]] * 2, axis=1)
        sine = jnp.concatenate([sin_ref[at, :]] * 2, axis=1)
        return nn(rows, weight_ref[...]) * cosine + nn(rows, swap_ref[...]) * sine

    ones = jnp.ones((16, BLOCK), BF16)

    def key_value(g, j):
        rows = norm_ref[g]
        k_ref[g] = turn(rows, wk_ref, wks_ref, j).astype(BF16)
        value_t = nt(wvt_ref[...], rows).astype(BF16)
        for pair in range(HEADS // 2):
            low = 2 * pair * head_dim
            v_ref[g, pair] = jnp.concatenate(
                [value_t[low : low + 2 * head_dim], ones], axis=0
            )

    def own(j, carry):
        q_ref[j] = (turn(norm_ref[blocks + j], wq_ref, wqs_ref, j) * scale).astype(BF16)
        key_value(blocks + j, j)
        return carry

    lax.fori_loop(0, blocks, own, 0)

    first = (tile - 1) * blocks
    total_blocks = tiles * blocks

    def place(b, m):
        entry = nbr_ref[b, m]
        offset = entry - first
        offset = jnp.where(offset < 0, offset + total_blocks, offset)
        offset = jnp.where(offset >= total_blocks, offset - total_blocks, offset)
        offset = jnp.minimum(offset, 3 * blocks - 1)
        return jnp.where(entry < 0, blocks + b, offset)

    last_rows = (NEIGHBOUR_COUNT - 1) * BLOCK

    def attend(b):
        places = [place(b, m) for m in range(NEIGHBOUR_COUNT)]
        bias = jnp.where(nbr_ref[b, NEIGHBOUR_COUNT - 1] < 0, NEG, 0.0).astype(F32)
        for m in range(NEIGHBOUR_COUNT):
            kc_ref[m * BLOCK : (m + 1) * BLOCK, :] = k_ref[places[m]]
        query = q_ref[b]
        for pair in range(HEADS // 2):
            slot = pair % 2
            scores = nt(kc_ref[...], head_pair(query, pair, head_dim))
            s_ref[slot] = scores
            tail = s_ref[slot, last_rows:, :] + bias
            top = jnp.maximum(
                jnp.max(scores[:last_rows], axis=0, keepdims=True),
                jnp.max(tail, axis=0, keepdims=True),
            )
            weights = jnp.concatenate(
                [
                    jnp.exp2(s_ref[slot, :last_rows, :] - top).astype(BF16),
                    jnp.exp2(tail - top).astype(BF16),
                ],
                axis=0,
            )
            held = jnp.concatenate([v_ref[g, pair] for g in places], axis=1)
            low = 2 * pair * head_dim
            att_ref[low : low + 2 * head_dim, :] = pair_result(
                nn(held, weights), head_dim, BLOCK
            )
        attended = att_ref[...].T.astype(BF16)
        at = pl.ds(pl.multiple_of(b * BLOCK, BLOCK), BLOCK)
        out_ref[at, :] = (mid_ref[b].astype(F32) + nn(attended, wo_ref[...])).astype(BF16)

    def arrive(j, carry):
        to_left(j).wait_recv()
        key_value(2 * blocks + j, j)
        to_right(blocks - 1 - j).wait_recv()
        key_value(blocks - 1 - j, blocks - 1 - j)
        return carry

    half = blocks // 2
    lax.fori_loop(0, half + 1, arrive, 0)

    def attend_pair(i, carry):
        attend(half - 1 - i)
        lax.fori_loop(half + 1 + i, jnp.minimum(half + 2 + i, blocks), arrive, 0)
        attend(half + i)
        return carry

    lax.fori_loop(0, half, attend_pair, 0)

    def sent(j, carry):
        to_left(j).wait_send()
        to_right(blocks - 1 - j).wait_send()
        return carry

    lax.fori_loop(0, blocks, sent, 0)


def rotary_tables(tokens, head_dim):
    half = head_dim // 2
    freqs = np.power(np.float32(10000.0), -np.arange(half, dtype=np.float32) / np.float32(half))
    angle = np.arange(tokens, dtype=np.float32)[:, None] * freqs[None, :].astype(np.float32)
    angle = np.tile(angle.astype(np.float64), (1, BLOCK // half))
    return np.cos(angle).astype(np.float32), np.sin(angle).astype(np.float32)


def space_attend(neighbours, state, returned, wt, gain, wq, wk, wv, wo):
    tokens, width = state.shape
    blocks = tokens // BLOCK
    head_dim = width // HEADS
    cosine, sine = rotary_tables(tokens, head_dim)
    vmem = pl.BlockSpec(memory_space=pltpu.VMEM)
    return pl.pallas_call(
        space_kernel,
        out_shape=jax.ShapeDtypeStruct(state.shape, BF16),
        in_specs=[pl.BlockSpec(memory_space=pltpu.SMEM)] + [vmem] * 10,
        out_specs=vmem,
        scratch_shapes=[
            pltpu.VMEM((3 * blocks, BLOCK, width), BF16),
            pltpu.VMEM((blocks, BLOCK, width), BF16),
            pltpu.VMEM((blocks, BLOCK, width), BF16),
            pltpu.VMEM((3 * blocks, BLOCK, width), BF16),
            pltpu.VMEM((3 * blocks, HEADS // 2, 2 * head_dim + 16, BLOCK), BF16),
            pltpu.VMEM((width, width), BF16),
            pltpu.VMEM((width, width), BF16),
            pltpu.VMEM((width, width), BF16),
            pltpu.VMEM((NEIGHBOUR_COUNT * BLOCK, width), BF16),
            pltpu.VMEM((2, NEIGHBOUR_COUNT * BLOCK, 2 * BLOCK), F32),
            pltpu.VMEM((width, BLOCK), F32),
            pltpu.SemaphoreType.DMA((blocks,)),
            pltpu.SemaphoreType.DMA((blocks,)),
            pltpu.SemaphoreType.DMA((blocks,)),
            pltpu.SemaphoreType.DMA((blocks,)),
        ],
        compiler_params=pltpu.CompilerParams(
            vmem_limit_bytes=48 << 20, collective_id=1, has_side_effects=True
        ),
    )(
        neighbours,
        state,
        returned,
        wt,
        gain.reshape(1, width),
        wq,
        wk,
        wv,
        wo,
        jnp.asarray(cosine),
        jnp.asarray(sine),
    )


def body(
    state_tokens,
    gain_time,
    query_time,
    key_time,
    value_time,
    output_time,
    gain_space,
    query_space,
    key_space,
    value_space,
    output_space,
    neighbours,
):
    frames_here, tokens_here, features = state_tokens.shape
    frame_count = lax.axis_size("frame")
    part = tokens_here // frame_count
    split_rows = state_tokens.reshape(frames_here, frame_count, part, features)
    shard_rows = lax.all_to_all(split_rows, "frame", split_axis=1, concat_axis=0, tiled=True)
    attended = time_attend(
        shard_rows.reshape(frame_count, part, features), gain_time, query_time, key_time, value_time
    )
    returned = lax.all_to_all(
        attended.reshape(frame_count, 1, part, features),
        "frame",
        split_axis=0,
        concat_axis=1,
        tiled=True,
    )
    updated = space_attend(
        neighbours,
        state_tokens.reshape(tokens_here, features),
        returned.reshape(tokens_here, features),
        output_time,
        gain_space,
        query_space,
        key_space,
        value_space,
        output_space,
    )
    return updated.reshape(state_tokens.shape)


def solution(mesh):
    return jax.shard_map(
        body,
        mesh=mesh,
        in_specs=(P("frame", "tile", None),) + (P(),) * 10 + (P("tile", None),),
        out_specs=P("frame", "tile", None),
        check_vma=False,
    )
```

time: 279 us -> 133 us (0.48)
  matrix products: 128 us -> 0 us
  Pallas kernels: 0 us -> 51 us
  local copies, waits for them, and re-layouts: 40.6 us -> 2.14 us
  waiting for transfers between devices: 28.9 us -> 0 us
  blocking collectives: 51.6 us -> 79 us
  starting transfers between devices: 19.1 us -> 0 us
  other arithmetic: 5.15 us -> 0 us
  loops' own time: 4.26 us -> 0 us
    sub x17 -> x0, matrix products: 68.1 us -> none  [the longest x16 62.5 us: attend_group(): weights = jax.nn.softmax(scores, axis=-1).astype(jnp.bfloat16)]
    dot_general x25 -> x0, matrix products: 59.9 us -> none  [the longest x16 49.7 us: attend_group(): jnp.einsum('fbqk,fbkd->fbqd', weights, gathered_values[..., lower:upper],...]
    pallas_call x0 -> x2, Pallas kernels: none -> 51 us  [the longest x1 41.4 us: space_attend(): pl.pallas_call(space_kernel, out_shape=jax.ShapeDtypeStruct(state.shape,...]
    all_to_all x0 -> x1, blocking collectives: none -> 27.1 us  [body(): lax.all_to_all(attended.reshape(frame_count, 1, part, features), 'frame',...]
    all_to_all x1 -> x0, waiting for transfers between devices: 20.5 us -> none  [body(): lax.all_to_all(gathered, 'frame', split_axis=0, concat_axis=1, tiled=True)]
    ppermute x2 -> x0, starting transfers between devices: 13.5 us -> none  [the longest x1 11.6 us: padded(): before = lax.ppermute(last, axis, up)]
    reshape x4 -> x0, local copies, waits for them, and re-layouts: 12.9 us -> none  [the longest x1 3.93 us: body(): t_key = project_rows(flat_rows, key_time).astype(jnp.bfloat16).reshape(fr...]
    gather x4 -> x0, local copies, waits for them, and re-layouts: 9.12 us -> none  [the longest x2 4.58 us: attend_group(): key_blocks[:, block_ids]]
  transfers between devices with their start and end apart: 3 -> 0, of which waited for: 3 -> 0; matrix products, arithmetic and copies ran while one was open for 1% -> 0% of each run, Pallas kernels for 0% -> 0%
where the time goes in v1:
time: 133 us; the launch traced here: 132 us
  blocking collectives  79 us (59%)
  Pallas kernels  51 us (38%)
  local copies, waits for them, and re-layouts  2.14 us (2%)
    all_to_all x1, blocking collectives, body(): lax.all_to_all(split_rows, 'frame', split_axis=1, concat_axis=0, tiled=True)  52 us
    pallas_call x1, Pallas kernels, space_attend(): pl.pallas_call(space_kernel, out_shape=jax.ShapeDtypeStruct(state.shape,...  41.4 us
    all_to_all x1, blocking collectives, body(): lax.all_to_all(attended.reshape(frame_count, 1, part, features), 'frame',...  27.1 us
    pallas_call x1, Pallas kernels, time_attend(): pl.pallas_call(time_kernel, out_shape=jax.ShapeDtypeStruct(rows.shape, BF...  9.67 us

profile of v1, /device:TPU:63, one launch (start us, length us, event | category | flops | bytes accessed | tf_op | source)
XLA Modules:
  0.0 132.3 jit_solution(9914846469481479147)
XLA Ops:
  0.0 0.0 copy-start.3
  0.0 0.0 copy-start.4
  0.0 0.0 copy-start.5
  0.0 52.0 %all_to_all.8 = bf16[1,16,64,256]{3,2,0,1:T(8,128)(2,1)S(1)} all-to-all(bf16[1,16,64,256]{3,2,0,1:T(8,128)(2,1)} %bitcast.12), channel_id=1, replica_groups=mesh['frame'=16,'tile'=32] {'frame'}, dimensions={1} | all-to-all | bytes 1048576 | tf_op jit(solution)/shard_map/all_to_all | solution.py:374
  52.0 0.0 copy-start.12
  52.0 0.0 copy-done.3
  52.0 0.0 copy-done.4
  52.0 0.0 copy-done.5
  52.0 0.7 copy-done.12
  52.7 0.0 copy-start.2
  52.7 0.0 copy-start.6
  52.7 0.0 copy-start.7
  52.7 0.0 copy-start.8
  52.7 0.0 copy-start.9
  52.7 0.0 copy-start.10
  52.7 9.7 %shard_map.136 = bf16[16,64,256]{2,1,0:T(8,128)(2,1)S(1)} custom-call(bf16[16,64,256]{2,1,0:T(8,128)(2,1)S(1)} %bitcast.11, f32[1,256]{1,0:T(1,128)S(1)} %bitcast.16, bf16[256,256]{1,0:T(8,128)(2,1)S(1)} %copy-done.3, bf16[256,256]{1,0:T(8,128)(2,1)S(1)} %copy-done.4, bf16[256,256]{1,0:T(8,128)(2,1)S(1)} %copy-done.5), custom_call_target="tpu_custom_call" | custom-call | tf_op jit(solution)/shard_map/pallas_call | solution.py:100
  62.4 0.0 copy-start
  62.4 0.0 copy-start.1
  62.4 27.1 %all_to_all.9 = bf16[16,1,64,256]{3,2,1,0:T(8,128)(2,1)S(1)} all-to-all(bf16[16,1,64,256]{3,2,1,0:T(8,128)(2,1)S(1)} %bitcast.10), channel_id=1, replica_groups=mesh['frame'=16,'tile'=32] {'frame'}, dimensions={0} | all-to-all | bytes 1048576 | tf_op jit(solution)/shard_map/all_to_all | solution.py:378
  89.5 0.0 copy-start.11
  89.5 0.0 copy-start.13
  89.5 0.0 copy-done.2
  89.5 0.0 copy-done.6
  89.5 0.0 copy-done.7
  89.5 0.0 copy-done.8
  89.5 0.0 copy-done.9
  89.5 0.0 copy-done.10
  89.5 0.0 copy-done
  89.5 0.0 copy-done.1
  89.6 0.6 copy-done.11
  90.2 0.0 copy-done.13
  90.2 41.4 %shard_map.137 = bf16[1024,256]{1,0:T(8,128)(2,1)S(1)} custom-call(s32[8,9]{1,0:T(8,128)S(1)} %copy-done.11, bf16[1024,256]{1,0:T(8,128)(2,1)S(1)} %bitcast.13, bf16[1024,256]{1,0:T(8,128)(2,1)S(1)} %bitcast.14, bf16[256,256]{1,0:T(8,128)(2,1)S(1)} %copy-done.6, f32[1,256]{1,0:T(1,128)S(1)} %bitcast.17, bf16[256,256]{1,0:T(8,128)(2,1)S(1)} %copy-done.7, ...), custom_call_target="tpu_custom_call" | custom-call | tf_op jit(solution)/shard_map/pallas_call | solution.py:316
  131.5 0.8 copy.17
Async XLA Ops:
  0.0 52.0 %copy-start.3 = (bf16[256,256]{1,0:T(8,128)(2,1)S(1)}, bf16[256,256]{1,0:T(8,128)(2,1)}, u32[]{:S(2)}) copy-start(bf16[256,256]{1,0:T(8,128)(2,1)} %wq_ref.2) | copy-start | bytes 393220
  0.0 52.0 %copy-start.4 = (bf16[256,256]{1,0:T(8,128)(2,1)S(1)}, bf16[256,256]{1,0:T(8,128)(2,1)}, u32[]{:S(2)}) copy-start(bf16[256,256]{1,0:T(8,128)(2,1)} %wk_ref.2) | copy-start | bytes 393220
  0.0 52.0 %copy-start.5 = (bf16[256,256]{1,0:T(8,128)(2,1)S(1)}, bf16[256,256]{1,0:T(8,128)(2,1)}, u32[]{:S(2)}) copy-start(bf16[256,256]{1,0:T(8,128)(2,1)} %wv_ref.2) | copy-start | bytes 393220
  52.0 0.7 copy-start.12
  52.7 36.8 %copy-start.2 = (f32[1024,128]{1,0:T(8,128)S(1)}, f32[1024,128]{1,0:T(8,128)}, u32[]{:S(2)}) copy-start(f32[1024,128]{1,0:T(8,128)} %constant.4.clone.cos_ref) | copy-start | bytes 1572868
  52.7 36.8 %copy-start.6 = (bf16[256,256]{1,0:T(8,128)(2,1)S(1)}, bf16[256,256]{1,0:T(8,128)(2,1)}, u32[]{:S(2)}) copy-start(bf16[256,256]{1,0:T(8,128)(2,1)} %wt_ref.1) | copy-start | bytes 393220
  52.7 36.8 %copy-start.7 = (bf16[256,256]{1,0:T(8,128)(2,1)S(1)}, bf16[256,256]{1,0:T(8,128)(2,1)}, u32[]{:S(2)}) copy-start(bf16[256,256]{1,0:T(8,128)(2,1)} %wq_ref.3) | copy-start | bytes 393220
  52.7 36.8 %copy-start.8 = (bf16[256,256]{1,0:T(8,128)(2,1)S(1)}, bf16[256,256]{1,0:T(8,128)(2,1)}, u32[]{:S(2)}) copy-start(bf16[256,256]{1,0:T(8,128)(2,1)} %wk_ref.3) | copy-start | bytes 393220
  52.7 36.8 %copy-start.9 = (bf16[256,256]{1,0:T(8,128)(2,1)S(1)}, bf16[256,256]{1,0:T(8,128)(2,1)}, u32[]{:S(2)}) copy-start(bf16[256,256]{1,0:T(8,128)(2,1)} %wv_ref.3) | copy-start | bytes 393220
  52.7 36.8 %copy-start.10 = (bf16[256,256]{1,0:T(8,128)(2,1)S(1)}, bf16[256,256]{1,0:T(8,128)(2,1)}, u32[]{:S(2)}) copy-start(bf16[256,256]{1,0:T(8,128)(2,1)} %wo_ref.1) | copy-start | bytes 393220
  62.4 27.1 %copy-start = (bf16[1,1024,256]{2,1,0:T(8,128)(2,1)S(1)}, bf16[1,1024,256]{2,1,0:T(8,128)(2,1)}, u32[]{:S(2)}) copy-start(bf16[1,1024,256]{2,1,0:T(8,128)(2,1)} %param.14) | copy-start | bytes 1572868
  62.4 27.1 %copy-start.1 = (f32[1024,128]{1,0:T(8,128)S(1)}, f32[1024,128]{1,0:T(8,128)}, u32[]{:S(2)}) copy-start(f32[1024,128]{1,0:T(8,128)} %constant.5.clone.sin_ref) | copy-start | bytes 1572868
  89.5 0.7 copy-start.11
  89.5 0.7 copy-start.13

commit v2 on v1

--- a/solution.py
+++ b/solution.py
@@ -49,53 +49,75 @@
     )
 
 
-def time_kernel(x_ref, gain_ref, wq_ref, wk_ref, wv_ref, out_ref, norm_ref, att_ref):
+def time_kernel(
+    x_ref, gain_ref, wq_ref, wk_ref, wv_ref, out_ref, q_ref, k_ref, v_ref
+):
     frames, tokens, width = x_ref.shape
     head_dim = width // HEADS
     scale = math.log2(math.e) / math.sqrt(head_dim)
     step = BLOCK // frames
     gain = gain_ref[...]
-
-    def norm_frame(f, carry):
-        norm_ref[f] = rms(x_ref[f].astype(F32), gain)
-        return carry
-
-    lax.fori_loop(0, frames, norm_frame, 0)
     wv_t = wv_ref[...].astype(F32).T.astype(BF16)
+
+    def at(i):
+        return pl.ds(pl.multiple_of(i * 2 * step, 2 * step), 2 * step)
+
+    def project(i, carry):
+        normed = rms(x_ref[:, at(i), :].astype(F32), gain)
+        rows = jnp.concatenate(
+            [
+                normed[:, k * step : (k + 1) * step].reshape(BLOCK, width).astype(BF16)
+                for k in range(2)
+            ],
+            axis=0,
+        )
+        query = (nn(rows, wq_ref[...]) * scale).astype(BF16)
+        key = nn(rows, wk_ref[...]).astype(BF16)
+        value_t = nt(wv_t, rows).astype(BF16)
+        q_ref[pl.ds(2 * i, 2)] = query.reshape(2, BLOCK, width)
+        k_ref[pl.ds(2 * i, 2)] = key.reshape(2, BLOCK, width)
+        for k in range(2):
+            v_ref[2 * i + k] = value_t[:, k * BLOCK : (k + 1) * BLOCK]
+        return carry
+
+    pairs = tokens // step // 2
+    lax.fori_loop(0, pairs, project, 0)
+
     row = lax.broadcasted_iota(jnp.int32, (BLOCK, 2 * BLOCK), 0)
     column = lax.broadcasted_iota(jnp.int32, (BLOCK, 2 * BLOCK), 1)
     same = (row % step) == (column % step)
     ones = jnp.ones((16, BLOCK), BF16)
 
-    def chunk(i, carry):
-        at = pl.ds(pl.multiple_of(i * step, step), step)
-        rows = norm_ref[:, at, :].reshape(BLOCK, width).astype(BF16)
-        query = (nn(rows, wq_ref[...]) * scale).astype(BF16)
-        key = nn(rows, wk_ref[...]).astype(BF16)
-        value_t = nt(wv_t, rows).astype(BF16)
-        parts = []
-        for pair in range(HEADS // 2):
-            scores = nt(key, head_pair(query, pair, head_dim))
-            scores = jnp.where(same, scores, NEG)
-            top = jnp.max(scores, axis=0, keepdims=True)
-            weights = jnp.exp2(scores - top).astype(BF16)
-            low = 2 * pair * head_dim
-            held = jnp.concatenate([value_t[low : low + 2 * head_dim], ones], axis=0)
-            parts.append(pair_result(nn(held, weights), head_dim, BLOCK))
-        att_ref[:, at, :] = jnp.concatenate(parts, axis=0).T.reshape(frames, step, width)
-        return carry
-
-    lax.fori_loop(0, tokens // step, chunk, 0)
-
-    def round_frame(f, carry):
-        out_ref[f] = att_ref[f].astype(BF16)
-        return carry
-
-    lax.fori_loop(0, frames, round_frame, 0)
+    def attend(i, carry):
+        halves = []
+        units = [(k, pair) for k in range(2) for pair in range(HEADS // 2)]
+        scores = {
+            (k, pair): jnp.where(
+                same, nt(k_ref[2 * i + k], head_pair(q_ref[2 * i + k], pair, head_dim)), NEG
+            )
+            for k, pair in units
+        }
+        weights = {
+            unit: jnp.exp2(value - jnp.max(value, axis=0, keepdims=True)).astype(BF16)
+            for unit, value in scores.items()
+        }
+        for k in range(2):
+            value_t = v_ref[2 * i + k]
+            parts = []
+            for pair in range(HEADS // 2):
+                low = 2 * pair * head_dim
+                held = jnp.concatenate([value_t[low : low + 2 * head_dim], ones], axis=0)
+                parts.append(pair_result(nn(held, weights[k, pair]), head_dim, BLOCK))
+            halves.append(jnp.concatenate(parts, axis=0).T.reshape(frames, step, width))
+        out_ref[:, at(i), :] = jnp.concatenate(halves, axis=1).astype(BF16)
+        return carry
+
+    lax.fori_loop(0, pairs, attend, 0)
 
 
 def time_attend(rows, gain, wq, wk, wv):
     frames, tokens, width = rows.shape
+    chunks = frames * tokens // BLOCK
     vmem = pl.BlockSpec(memory_space=pltpu.VMEM)
     return pl.pallas_call(
         time_kernel,
@@ -103,8 +125,9 @@
         in_specs=[vmem] * 5,
         out_specs=vmem,
         scratch_shapes=[
-            pltpu.VMEM(rows.shape, F32),
-            pltpu.VMEM(rows.shape, F32),
+            pltpu.VMEM((chunks, BLOCK, width), BF16),
+            pltpu.VMEM((chunks, BLOCK, width), BF16),
+            pltpu.VMEM((chunks, width, BLOCK), BF16),
         ],
         compiler_params=pltpu.CompilerParams(vmem_limit_bytes=32 << 20),
     )(rows, gain.reshape(1, width), wq, wk, wv)
@@ -138,10 +161,11 @@
     q_ref,
     k_ref,
     v_ref,
-    wqs_ref,
-    wks_ref,
+    wq2_ref,
+    wk2_ref,
     wvt_ref,
-    kc_ref,
+    kca_ref,
+    kcb_ref,
     s_ref,
     att_ref,
     send_l,
@@ -200,34 +224,41 @@
 
     lax.fori_loop(0, blocks, send, 0)
 
-    wqs_ref[...] = swapped(wq_ref[...])
-    wks_ref[...] = swapped(wk_ref[...])
+    wq2_ref[:, :width] = wq_ref[...]
+    wq2_ref[:, width:] = swapped(wq_ref[...])
+    wk2_ref[:, :width] = wk_ref[...]
+    wk2_ref[:, width:] = swapped(wk_ref[...])
     wvt_ref[...] = wv_ref[...].astype(F32).T.astype(BF16)
 
-    def turn(rows, weight_ref, swap_ref, j):
-        at = pl.ds(pl.multiple_of(j * BLOCK, BLOCK), BLOCK)
+    def turn(rows, weight_ref, j):
+        at = pl.ds(pl.multiple_of(j * BLOCK, BLOCK), 2 * BLOCK)
         cosine = jnp.concatenate([cos_ref[at, :]] * 2, axis=1)
         sine = jnp.concatenate([sin_ref[at, :]] * 2, axis=1)
-        return nn(rows, weight_ref[...]) * cosine + nn(rows, swap_ref[...]) * sine
+        both = nn(rows, weight_ref[...])
+        return both[:, :width] * cosine + both[:, width:] * sine
 
     ones = jnp.ones((16, BLOCK), BF16)
 
     def key_value(g, j):
-        rows = norm_ref[g]
-        k_ref[g] = turn(rows, wk_ref, wks_ref, j).astype(BF16)
+        rows = norm_ref[pl.ds(g, 2)].reshape(2 * BLOCK, width)
+        k_ref[pl.ds(g, 2)] = turn(rows, wk2_ref, j).astype(BF16).reshape(2, BLOCK, width)
         value_t = nt(wvt_ref[...], rows).astype(BF16)
         for pair in range(HEADS // 2):
             low = 2 * pair * head_dim
-            v_ref[g, pair] = jnp.concatenate(
-                [value_t[low : low + 2 * head_dim], ones], axis=0
-            )
-
-    def own(j, carry):
-        q_ref[j] = (turn(norm_ref[blocks + j], wq_ref, wqs_ref, j) * scale).astype(BF16)
+            for k in range(2):
+                v_ref[g + k, pair] = jnp.concatenate(
+                    [value_t[low : low + 2 * head_dim, k * BLOCK : (k + 1) * BLOCK], ones], axis=0
+                )
+
+    def own(i, carry):
+        j = 2 * i
+        rows = norm_ref[pl.ds(blocks + j, 2)].reshape(2 * BLOCK, width)
+        query = (turn(rows, wq2_ref, j) * scale).astype(BF16)
+        q_ref[pl.ds(j, 2)] = query.reshape(2, BLOCK, width)
         key_value(blocks + j, j)
         return carry
 
-    lax.fori_loop(0, blocks, own, 0)
+    lax.fori_loop(0, blocks // 2, own, 0)
 
     first = (tile - 1) * blocks
     total_blocks = tiles * blocks
@@ -240,56 +271,80 @@
         offset = jnp.minimum(offset, 3 * blocks - 1)
         return jnp.where(entry < 0, blocks + b, offset)
 
+    def places(b):
+        return [place(b, m) for m in range(NEIGHBOUR_COUNT)]
+
     last_rows = (NEIGHBOUR_COUNT - 1) * BLOCK
 
-    def attend(b):
-        places = [place(b, m) for m in range(NEIGHBOUR_COUNT)]
-        bias = jnp.where(nbr_ref[b, NEIGHBOUR_COUNT - 1] < 0, NEG, 0.0).astype(F32)
+    def bias_of(b):
+        return jnp.where(nbr_ref[b, NEIGHBOUR_COUNT - 1] < 0, NEG, 0.0).astype(F32)
+
+    def fill(kc_ref, at):
         for m in range(NEIGHBOUR_COUNT):
-            kc_ref[m * BLOCK : (m + 1) * BLOCK, :] = k_ref[places[m]]
+            kc_ref[m * BLOCK : (m + 1) * BLOCK, :] = k_ref[at[m]]
+
+    def score(kc_ref, query, pair, bias):
+        scores = nt(kc_ref[...], head_pair(query, pair, head_dim))
+        tail = scores[last_rows:] + bias
+        s_ref[pair, :last_rows, :] = scores[:last_rows]
+        s_ref[pair, last_rows:, :] = tail
+        return jnp.maximum(
+            jnp.max(scores[:last_rows], axis=0, keepdims=True),
+            jnp.max(tail, axis=0, keepdims=True),
+        )
+
+    def weigh(at, pair, top):
+        weights = jnp.exp2(s_ref[pair] - top).astype(BF16)
+        held = jnp.concatenate([v_ref[g, pair] for g in at], axis=1)
+        low = 2 * pair * head_dim
+        att_ref[low : low + 2 * head_dim, :] = pair_result(nn(held, weights), head_dim, BLOCK)
+
+    def arrive(i, carry):
+        j = 2 * i
+        for k in range(2):
+            to_left(j + k).wait_recv()
+            to_right(blocks - 1 - j - k).wait_recv()
+        key_value(2 * blocks + j, j)
+        key_value(blocks - 2 - j, blocks - 2 - j)
+        return carry
+
+    lax.fori_loop(0, blocks // 2, arrive, 0)
+
+    def attend(b, tops):
+        here = places(b)
+        after = jnp.minimum(b + 1, blocks - 1)
+        there = places(after)
         query = q_ref[b]
-        for pair in range(HEADS // 2):
-            slot = pair % 2
-            scores = nt(kc_ref[...], head_pair(query, pair, head_dim))
-            s_ref[slot] = scores
-            tail = s_ref[slot, last_rows:, :] + bias
-            top = jnp.maximum(
-                jnp.max(scores[:last_rows], axis=0, keepdims=True),
-                jnp.max(tail, axis=0, keepdims=True),
-            )
-            weights = jnp.concatenate(
-                [
-                    jnp.exp2(s_ref[slot, :last_rows, :] - top).astype(BF16),
-                    jnp.exp2(tail - top).astype(BF16),
-                ],
-                axis=0,
-            )
-            held = jnp.concatenate([v_ref[g, pair] for g in places], axis=1)
-            low = 2 * pair * head_dim
-            att_ref[low : low + 2 * head_dim, :] = pair_result(
-                nn(held, weights), head_dim, BLOCK
-            )
+        bias = bias_of(b)
+        fill(kca_ref, there)
+        query_after = q_ref[after]
+        bias_after = bias_of(after)
+        late = [score(kcb_ref, query, 2, bias)]
+        weigh(here, 0, tops[0])
+        late.append(score(kcb_ref, query, 3, bias))
+        weigh(here, 1, tops[1])
+        fill(kcb_ref, there)
+        early = [score(kca_ref, query_after, 0, bias_after)]
+        weigh(here, 2, late[0])
+        early.append(score(kca_ref, query_after, 1, bias_after))
+        weigh(here, 3, late[1])
+        early = tuple(early)
         attended = att_ref[...].T.astype(BF16)
         at = pl.ds(pl.multiple_of(b * BLOCK, BLOCK), BLOCK)
         out_ref[at, :] = (mid_ref[b].astype(F32) + nn(attended, wo_ref[...])).astype(BF16)
-
-    def arrive(j, carry):
-        to_left(j).wait_recv()
-        key_value(2 * blocks + j, j)
-        to_right(blocks - 1 - j).wait_recv()
-        key_value(blocks - 1 - j, blocks - 1 - j)
-        return carry
-
-    half = blocks // 2
-    lax.fori_loop(0, half + 1, arrive, 0)
-
-    def attend_pair(i, carry):
-        attend(half - 1 - i)
-        lax.fori_loop(half + 1 + i, jnp.minimum(half + 2 + i, blocks), arrive, 0)
-        attend(half + i)
-        return carry
-
-    lax.fori_loop(0, half, attend_pair, 0)
+        return early
+
+    at_first = places(0)
+    fill(kca_ref, at_first)
+    fill(kcb_ref, at_first)
+    query_first = q_ref[0]
+    bias_first = bias_of(0)
+    lax.fori_loop(
+        0,
+        blocks,
+        attend,
+        tuple(score(kca_ref, query_first, pair, bias_first) for pair in (0, 1)),
+    )
 
     def sent(j, carry):
         to_left(j).wait_send()
@@ -324,11 +379,12 @@
             pltpu.VMEM((blocks, BLOCK, width), BF16),
             pltpu.VMEM((3 * blocks, BLOCK, width), BF16),
             pltpu.VMEM((3 * blocks, HEADS // 2, 2 * head_dim + 16, BLOCK), BF16),
-            pltpu.VMEM((width, width), BF16),
-            pltpu.VMEM((width, width), BF16),
+            pltpu.VMEM((width, 2 * width), BF16),
+            pltpu.VMEM((width, 2 * width), BF16),
             pltpu.VMEM((width, width), BF16),
             pltpu.VMEM((NEIGHBOUR_COUNT * BLOCK, width), BF16),
-            pltpu.VMEM((2, NEIGHBOUR_COUNT * BLOCK, 2 * BLOCK), F32),
+            pltpu.VMEM((NEIGHBOUR_COUNT * BLOCK, width), BF16),
+            pltpu.VMEM((HEADS // 2, NEIGHBOUR_COUNT * BLOCK, 2 * BLOCK), F32),
             pltpu.VMEM((width, BLOCK), F32),
             pltpu.SemaphoreType.DMA((blocks,)),
             pltpu.SemaphoreType.DMA((blocks,)),

time: 133 us -> 118 us (0.89)
  the two profiles are of different devices: /device:TPU:63 before, /device:TPU:71 now
where the time goes in v2:
time: 118 us
  blocking collectives  87.4 us (74%)
  Pallas kernels  28.5 us (24%)
  local copies, waits for them, and re-layouts  2.14 us (2%)
    all_to_all x1, blocking collectives, body(): lax.all_to_all(attended.reshape(frame_count, 1, part, features), 'frame',...  43.9 us
    all_to_all x1, blocking collectives, body(): lax.all_to_all(split_rows, 'frame', split_axis=1, concat_axis=0, tiled=True)  43.5 us
    pallas_call x1, Pallas kernels, space_attend(): pl.pallas_call(space_kernel, out_shape=jax.ShapeDtypeStruct(state.shape,...  23.7 us
    pallas_call x1, Pallas kernels, time_attend(): pl.pallas_call(time_kernel, out_shape=jax.ShapeDtypeStruct(rows.shape, BF...  4.78 us

profile of v2, /device:TPU:71, one launch (start us, length us, event | category | flops | bytes accessed | tf_op | source)
XLA Modules:
  0.0 118.2 jit_solution(13794438800890999292)
XLA Ops:
  0.0 0.0 copy-start.3
  0.0 0.0 copy-start.4
  0.0 0.0 copy-start.5
  0.0 43.5 %all_to_all.8 = bf16[1,16,64,256]{3,2,0,1:T(8,128)(2,1)S(1)} all-to-all(bf16[1,16,64,256]{3,2,0,1:T(8,128)(2,1)} %bitcast.12), channel_id=1, replica_groups=mesh['frame'=16,'tile'=32] {'frame'}, dimensions={1} | all-to-all | bytes 1048576 | tf_op jit(solution)/shard_map/all_to_all | solution.py:430
  43.5 0.0 copy-start.12
  43.6 0.0 copy-done.3
  43.6 0.0 copy-done.4
  43.6 0.0 copy-done.5
  43.6 0.7 copy-done.12
  44.2 0.0 copy-start.2
  44.2 0.0 copy-start.6
  44.2 0.0 copy-start.7
  44.2 0.0 copy-start.8
  44.2 0.0 copy-start.9
  44.3 0.0 copy-start.10
  44.3 4.8 %shard_map.136 = bf16[16,64,256]{2,1,0:T(8,128)(2,1)S(1)} custom-call(bf16[16,64,256]{2,1,0:T(8,128)(2,1)S(1)} %bitcast.11, f32[1,256]{1,0:T(1,128)S(1)} %bitcast.16, bf16[256,256]{1,0:T(8,128)(2,1)S(1)} %copy-done.3, bf16[256,256]{1,0:T(8,128)(2,1)S(1)} %copy-done.4, bf16[256,256]{1,0:T(8,128)(2,1)S(1)} %copy-done.5), custom_call_target="tpu_custom_call" | custom-call | tf_op jit(solution)/shard_map/pallas_call | solution.py:122
  49.1 0.0 copy-start
  49.1 0.0 copy-start.1
  49.1 43.9 %all_to_all.9 = bf16[16,1,64,256]{3,2,1,0:T(8,128)(2,1)S(1)} all-to-all(bf16[16,1,64,256]{3,2,1,0:T(8,128)(2,1)S(1)} %bitcast.10), channel_id=1, replica_groups=mesh['frame'=16,'tile'=32] {'frame'}, dimensions={0} | all-to-all | bytes 1048576 | tf_op jit(solution)/shard_map/all_to_all | solution.py:434
  92.9 0.0 copy-start.11
  92.9 0.0 copy-start.13
  92.9 0.0 copy-done.2
  92.9 0.0 copy-done.6
  93.0 0.0 copy-done.7
  93.0 0.0 copy-done.8
  93.0 0.0 copy-done.9
  93.0 0.0 copy-done.10
  93.0 0.0 copy-done
  93.0 0.0 copy-done.1
  93.0 0.6 copy-done.11
  93.6 0.0 copy-done.13
  93.6 23.7 %shard_map.137 = bf16[1024,256]{1,0:T(8,128)(2,1)S(1)} custom-call(s32[8,9]{1,0:T(8,128)S(1)} %copy-done.11, bf16[1024,256]{1,0:T(8,128)(2,1)S(1)} %bitcast.13, bf16[1024,256]{1,0:T(8,128)(2,1)S(1)} %bitcast.14, bf16[256,256]{1,0:T(8,128)(2,1)S(1)} %copy-done.6, f32[1,256]{1,0:T(1,128)S(1)} %bitcast.17, bf16[256,256]{1,0:T(8,128)(2,1)S(1)} %copy-done.7, ...), custom_call_target="tpu_custom_call" | custom-call | tf_op jit(solution)/shard_map/pallas_call | solution.py:371
  117.4 0.8 copy.17
Async XLA Ops:
  0.0 43.6 %copy-start.3 = (bf16[256,256]{1,0:T(8,128)(2,1)S(1)}, bf16[256,256]{1,0:T(8,128)(2,1)}, u32[]{:S(2)}) copy-start(bf16[256,256]{1,0:T(8,128)(2,1)} %wq_ref.2) | copy-start | bytes 393220
  0.0 43.6 %copy-start.4 = (bf16[256,256]{1,0:T(8,128)(2,1)S(1)}, bf16[256,256]{1,0:T(8,128)(2,1)}, u32[]{:S(2)}) copy-start(bf16[256,256]{1,0:T(8,128)(2,1)} %wk_ref.2) | copy-start | bytes 393220
  0.0 43.6 %copy-start.5 = (bf16[256,256]{1,0:T(8,128)(2,1)S(1)}, bf16[256,256]{1,0:T(8,128)(2,1)}, u32[]{:S(2)}) copy-start(bf16[256,256]{1,0:T(8,128)(2,1)} %wv_ref.2) | copy-start | bytes 393220
  43.5 0.7 copy-start.12
  44.2 48.7 %copy-start.2 = (f32[1024,128]{1,0:T(8,128)S(1)}, f32[1024,128]{1,0:T(8,128)}, u32[]{:S(2)}) copy-start(f32[1024,128]{1,0:T(8,128)} %constant.4.clone.cos_ref) | copy-start | bytes 1572868
  44.2 48.7 %copy-start.6 = (bf16[256,256]{1,0:T(8,128)(2,1)S(1)}, bf16[256,256]{1,0:T(8,128)(2,1)}, u32[]{:S(2)}) copy-start(bf16[256,256]{1,0:T(8,128)(2,1)} %wt_ref.1) | copy-start | bytes 393220
  44.2 48.7 %copy-start.7 = (bf16[256,256]{1,0:T(8,128)(2,1)S(1)}, bf16[256,256]{1,0:T(8,128)(2,1)}, u32[]{:S(2)}) copy-start(bf16[256,256]{1,0:T(8,128)(2,1)} %wq_ref.3) | copy-start | bytes 393220
  44.2 48.7 %copy-start.8 = (bf16[256,256]{1,0:T(8,128)(2,1)S(1)}, bf16[256,256]{1,0:T(8,128)(2,1)}, u32[]{:S(2)}) copy-start(bf16[256,256]{1,0:T(8,128)(2,1)} %wk_ref.3) | copy-start | bytes 393220
  44.2 48.7 %copy-start.9 = (bf16[256,256]{1,0:T(8,128)(2,1)S(1)}, bf16[256,256]{1,0:T(8,128)(2,1)}, u32[]{:S(2)}) copy-start(bf16[256,256]{1,0:T(8,128)(2,1)} %wv_ref.3) | copy-start | bytes 393220
  44.3 48.7 %copy-start.10 = (bf16[256,256]{1,0:T(8,128)(2,1)S(1)}, bf16[256,256]{1,0:T(8,128)(2,1)}, u32[]{:S(2)}) copy-start(bf16[256,256]{1,0:T(8,128)(2,1)} %wo_ref.1) | copy-start | bytes 393220
  49.1 43.9 %copy-start = (bf16[1,1024,256]{2,1,0:T(8,128)(2,1)S(1)}, bf16[1,1024,256]{2,1,0:T(8,128)(2,1)}, u32[]{:S(2)}) copy-start(bf16[1,1024,256]{2,1,0:T(8,128)(2,1)} %param.14) | copy-start | bytes 1572868
  49.1 43.9 %copy-start.1 = (f32[1024,128]{1,0:T(8,128)S(1)}, f32[1024,128]{1,0:T(8,128)}, u32[]{:S(2)}) copy-start(f32[1024,128]{1,0:T(8,128)} %constant.5.clone.sin_ref) | copy-start | bytes 1572868
  92.9 0.7 copy-start.11
  92.9 0.7 copy-start.13

commit v3 on v2

v3 whole, which is shorter than its diff:
```python
import functools
import math

import jax
import jax.numpy as jnp
import numpy as np
from jax import lax
from jax.experimental import pallas as pl
from jax.experimental.pallas import tpu as pltpu
from jax.sharding import PartitionSpec as P

HEADS = 8
BLOCK = 128
NEIGHBOUR_COUNT = 9
EPS = 1e-05
ROT_PERIOD = 1024
NEG = -1e30
F32 = jnp.float32
BF16 = jnp.bfloat16
MESH = pl.DeviceIdType.MESH


def nt(a, b):
    return lax.dot_general(a, b, (((1,), (1,)), ((), ())), preferred_element_type=F32)


def nn(a, b):
    return lax.dot_general(a, b, (((1,), (0,)), ((), ())), preferred_element_type=F32)


def rms(values, gain):
    square_mean = jnp.mean(values * values, axis=-1, keepdims=True)
    return values * lax.rsqrt(square_mean + EPS) * gain


def head_pair(rows, pair, head_dim):
    lane_head = lax.broadcasted_iota(jnp.int32, rows.shape, 1) // head_dim
    zero = jnp.zeros_like(rows)
    return jnp.concatenate(
        [jnp.where(lane_head == 2 * pair + k, rows, zero) for k in range(2)], axis=0
    )


def pair_result(total, head_dim, count):
    inverse = 1.0 / total[2 * head_dim : 2 * head_dim + 1, :]
    scaled = total[: 2 * head_dim, :] * inverse
    return jnp.concatenate(
        [scaled[:head_dim, :count], scaled[head_dim:, count:]], axis=0
    )


def time_chunk(slots, gain, wq, wk, wv_t, same, scale, head_dim):
    frames, tokens, width = slots.shape
    step = tokens // 2
    normed = rms(slots.astype(F32), gain)
    rows = jnp.concatenate(
        [
            normed[:, k * step : (k + 1) * step].reshape(BLOCK, width).astype(BF16)
            for k in range(2)
        ],
        axis=0,
    )
    query = (nn(rows, wq) * scale).astype(BF16)
    key = nn(rows, wk).astype(BF16)
    value_t = nt(wv_t, rows).astype(BF16)
    ones = jnp.ones((16, BLOCK), BF16)
    units = [(k, pair) for k in range(2) for pair in range(HEADS // 2)]
    scores = {}
    for k, pair in units:
        part = slice(k * BLOCK, (k + 1) * BLOCK)
        scores[k, pair] = jnp.where(
            same, nt(key[part], head_pair(query[part], pair, head_dim)), NEG
        )
    weights = {
        unit: jnp.exp2(value - jnp.max(value, axis=0, keepdims=True)).astype(BF16)
        for unit, value in scores.items()
    }
    halves = []
    for k in range(2):
        parts = []
        for pair in range(HEADS // 2):
            low = 2 * pair * head_dim
            held = jnp.concatenate(
                [value_t[low : low + 2 * head_dim, k * BLOCK : (k + 1) * BLOCK], ones], axis=0
            )
            parts.append(pair_result(nn(held, weights[k, pair]), head_dim, BLOCK))
        halves.append(jnp.concatenate(parts, axis=0).T.reshape(frames, step, width))
    return jnp.concatenate(halves, axis=1)


def swapped(weight):
    wide = weight.astype(F32)
    width = wide.shape[1]
    half = width // HEADS // 2
    lane = lax.broadcasted_iota(jnp.int32, wide.shape, 1)
    ahead = pltpu.roll(wide, width - half, 1)
    behind = pltpu.roll(wide, half, 1)
    return jnp.where(lane % (2 * half) < half, -ahead, behind).astype(BF16)


def layer_kernel(
    nbr_ref,
    state_ref,
    gain_t_ref,
    wqt_ref,
    wkt_ref,
    wvt_in_ref,
    wt_ref,
    gain_ref,
    wq_ref,
    wk_ref,
    wv_ref,
    wo_ref,
    cos_ref,
    sin_ref,
    out_ref,
    rows_ref,
    attn_ref,
    ret_ref,
    norm_ref,
    mid_ref,
    q_ref,
    k_ref,
    v_ref,
    wq2_ref,
    wk2_ref,
    wvt_ref,
    wvtt_ref,
    kca_ref,
    kcb_ref,
    s_ref,
    att_ref,
    go_sem,
    come_sem,
    back_sem,
    home_sem,
    send_l,
    recv_l,
    send_r,
    recv_r,
):
    blocks = mid_ref.shape[0]
    width = state_ref.shape[-1]
    head_dim = width // HEADS
    scale = math.log2(math.e) / math.sqrt(head_dim)
    chunks, frames, slab, _ = rows_ref.shape
    half = frames // 2
    per = blocks // chunks
    tile = lax.axis_index("tile")
    tiles = lax.axis_size("tile")
    left = lax.rem(tile + tiles - 1, tiles)
    right = lax.rem(tile + 1, tiles)
    me = lax.axis_index("frame")
    my_side = me // half
    my_place = lax.rem(me, half)

    def peer_at(k):
        return lax.rem(my_side + k // half, 2) * half + lax.rem(my_place + lax.rem(k, half), half)

    def mirror(k):
        return (k // half) * half + lax.rem(half - lax.rem(k, half), half)

    barrier = pltpu.get_barrier_semaphore()

    def greet(k, carry):
        pl.semaphore_signal(
            barrier, inc=1, device_id={"frame": peer_at(k)}, device_id_type=MESH
        )
        return carry

    lax.fori_loop(1, frames, greet, 0)
    for peer in (left, right):
        pl.semaphore_signal(barrier, inc=1, device_id={"tile": peer}, device_id_type=MESH)

    def go(c, k):
        at = pl.ds(pl.multiple_of((c * frames + peer_at(k)) * slab, slab), slab)
        return pltpu.make_async_remote_copy(
            src_ref=state_ref.at[at, :],
            dst_ref=rows_ref.at[c, mirror(k)],
            send_sem=go_sem.at[c],
            recv_sem=come_sem.at[c],
            device_id={"frame": peer_at(k)},
            device_id_type=MESH,
        )

    def back(c, k):
        return pltpu.make_async_remote_copy(
            src_ref=attn_ref.at[c, k],
            dst_ref=ret_ref.at[c, me],
            send_sem=back_sem.at[c],
            recv_sem=home_sem.at[c],
            device_id={"frame": peer_at(k)},
            device_id_type=MESH,
        )

    def whole(ref, c, send_sem, recv_sem):
        return pltpu.make_async_remote_copy(
            src_ref=ref.at[c, pl.ds(0, frames - 1)],
            dst_ref=ref.at[c, pl.ds(0, frames - 1)],
            send_sem=send_sem.at[c],
            recv_sem=recv_sem.at[c],
            device_id={"frame": peer_at(1)},
            device_id_type=MESH,
        )

    def to_left(c):
        return pltpu.make_async_remote_copy(
            src_ref=norm_ref.at[pl.ds(blocks + per * c, per)],
            dst_ref=norm_ref.at[pl.ds(2 * blocks + per * c, per)],
            send_sem=send_l.at[c],
            recv_sem=recv_l.at[c],
            device_id={"tile": left},
            device_id_type=MESH,
        )

    def to_right(c):
        return pltpu.make_async_remote_copy(
            src_ref=norm_ref.at[pl.ds(blocks + per * c, per)],
            dst_ref=norm_ref.at[pl.ds(per * c, per)],
            send_sem=send_r.at[c],
            recv_sem=recv_r.at[c],
            device_id={"tile": right},
            device_id_type=MESH,
        )

    pl.semaphore_wait(barrier, frames + 1)

    def leave(c, carry):
        def one(i, inner):
            go(c, frames - 1 - i).start()
            return inner

        return lax.fori_loop(0, frames - 1, one, carry)

    lax.fori_loop(0, chunks, leave, 0)

    def stay(c, carry):
        at = pl.ds(pl.multiple_of((c * frames + me) * slab, slab), slab)
        rows_ref[c, 0] = state_ref[at, :]
        return carry

    lax.fori_loop(0, chunks, stay, 0)
    wvtt_ref[...] = wvt_in_ref[...].astype(F32).T.astype(BF16)
    wq2_ref[:, :width] = wq_ref[...]
    wq2_ref[:, width:] = swapped(wq_ref[...])
    wk2_ref[:, :width] = wk_ref[...]
    wk2_ref[:, width:] = swapped(wk_ref[...])
    wvt_ref[...] = wv_ref[...].astype(F32).T.astype(BF16)


    row = lax.broadcasted_iota(jnp.int32, (BLOCK, 2 * BLOCK), 0)
    column = lax.broadcasted_iota(jnp.int32, (BLOCK, 2 * BLOCK), 1)
    step = slab // 2
    same = (row % step) == (column % step)

    def over_time(c, carry):
        whole(rows_ref, c, go_sem, come_sem).wait_recv()
        attended = time_chunk(
            rows_ref[c],
            gain_t_ref[...],
            wqt_ref[...],
            wkt_ref[...],
            wvtt_ref[...],
            same,
            scale,
            head_dim,
        )
        attn_ref[c] = attended.astype(BF16)

        def one(i, inner):
            back(c, frames - 1 - i).start()
            return inner

        lax.fori_loop(0, frames - 1, one, 0)
        ret_ref[c, me] = attn_ref[c, 0]
        return carry

    lax.fori_loop(0, chunks, over_time, 0)

    def turn(rows, weight_ref, j):
        at = pl.ds(pl.multiple_of(j * BLOCK, BLOCK), 2 * BLOCK)
        cosine = jnp.concatenate([cos_ref[at, :]] * 2, axis=1)
        sine = jnp.concatenate([sin_ref[at, :]] * 2, axis=1)
        both = nn(rows, weight_ref[...])
        return both[:, :width] * cosine + both[:, width:] * sine

    ones = jnp.ones((16, BLOCK), BF16)

    def key_value(g, j):
        rows = norm_ref[pl.ds(g, 2)].reshape(2 * BLOCK, width)
        k_ref[pl.ds(g, 2)] = turn(rows, wk2_ref, j).astype(BF16).reshape(2, BLOCK, width)
        value_t = nt(wvt_ref[...], rows).astype(BF16)
        for pair in range(HEADS // 2):
            low = 2 * pair * head_dim
            for k in range(2):
                v_ref[g + k, pair] = jnp.concatenate(
                    [value_t[low : low + 2 * head_dim, k * BLOCK : (k + 1) * BLOCK], ones], axis=0
                )

    gain = gain_ref[...]

    def own(c, carry):
        j = per * c
        whole(ret_ref, c, back_sem, home_sem).wait_recv()
        at = pl.ds(pl.multiple_of(c * frames * slab, frames * slab), frames * slab)
        returned = ret_ref[c].reshape(frames * slab, width)
        mid = (state_ref[at, :].astype(F32) + nn(returned, wt_ref[...])).astype(BF16)
        mid_ref[pl.ds(j, per)] = mid.reshape(per, BLOCK, width)
        rows = rms(mid.astype(F32), gain).astype(BF16)
        norm_ref[pl.ds(blocks + j, per)] = rows.reshape(per, BLOCK, width)
        to_left(c).start()
        to_right(c).start()
        query = (turn(rows, wq2_ref, j) * scale).astype(BF16)
        q_ref[pl.ds(j, per)] = query.reshape(per, BLOCK, width)
        key_value(blocks + j, j)
        return carry

    lax.fori_loop(0, chunks, own, 0)

    first = (tile - 1) * blocks
    total_blocks = tiles * blocks

    def place(b, m):
        entry = nbr_ref[b, m]
        offset = entry - first
        offset = jnp.where(offset < 0, offset + total_blocks, offset)
        offset = jnp.where(offset >= total_blocks, offset - total_blocks, offset)
        offset = jnp.minimum(offset, 3 * blocks - 1)
        return jnp.where(entry < 0, blocks + b, offset)

    def places(b):
        return [place(b, m) for m in range(NEIGHBOUR_COUNT)]

    last_rows = (NEIGHBOUR_COUNT - 1) * BLOCK

    def bias_of(b):
        return jnp.where(nbr_ref[b, NEIGHBOUR_COUNT - 1] < 0, NEG, 0.0).astype(F32)

    def fill(kc_ref, at):
        for m in range(NEIGHBOUR_COUNT):
            kc_ref[m * BLOCK : (m + 1) * BLOCK, :] = k_ref[at[m]]

    def score(kc_ref, query, pair, bias):
        scores = nt(kc_ref[...], head_pair(query, pair, head_dim))
        tail = scores[last_rows:] + bias
        s_ref[pair, :last_rows, :] = scores[:last_rows]
        s_ref[pair, last_rows:, :] = tail
        return jnp.maximum(
            jnp.max(scores[:last_rows], axis=0, keepdims=True),
            jnp.max(tail, axis=0, keepdims=True),
        )

    def weigh(at, pair, top):
        weights = jnp.exp2(s_ref[pair] - top).astype(BF16)
        held = jnp.concatenate([v_ref[g, pair] for g in at], axis=1)
        low = 2 * pair * head_dim
        att_ref[low : low + 2 * head_dim, :] = pair_result(nn(held, weights), head_dim, BLOCK)

    def arrive(c, carry):
        to_left(c).wait_recv()
        key_value(2 * blocks + per * c, per * c)
        to_right(c).wait_recv()
        key_value(per * c, per * c)
        return carry

    lax.fori_loop(0, chunks, arrive, 0)

    def attend(b, tops):
        here = places(b)
        after = jnp.minimum(b + 1, blocks - 1)
        there = places(after)
        query = q_ref[b]
        bias = bias_of(b)
        fill(kca_ref, there)
        query_after = q_ref[after]
        bias_after = bias_of(after)
        late = [score(kcb_ref, query, 2, bias)]
        weigh(here, 0, tops[0])
        late.append(score(kcb_ref, query, 3, bias))
        weigh(here, 1, tops[1])
        fill(kcb_ref, there)
        early = [score(kca_ref, query_after, 0, bias_after)]
        weigh(here, 2, late[0])
        early.append(score(kca_ref, query_after, 1, bias_after))
        weigh(here, 3, late[1])
        early = tuple(early)
        attended = att_ref[...].T.astype(BF16)
        at = pl.ds(pl.multiple_of(b * BLOCK, BLOCK), BLOCK)
        out_ref[at, :] = (mid_ref[b].astype(F32) + nn(attended, wo_ref[...])).astype(BF16)
        return early

    at_first = places(0)
    fill(kca_ref, at_first)
    fill(kcb_ref, at_first)
    query_first = q_ref[0]
    bias_first = bias_of(0)
    lax.fori_loop(
        0,
        blocks,
        attend,
        tuple(score(kca_ref, query_first, pair, bias_first) for pair in (0, 1)),
    )

    def sent(c, carry):
        whole(rows_ref, c, go_sem, come_sem).wait_send()
        whole(ret_ref, c, back_sem, home_sem).wait_send()
        to_left(c).wait_send()
        to_right(c).wait_send()
        return carry

    lax.fori_loop(0, chunks, sent, 0)


def rotary_tables(tokens, head_dim):
    half = head_dim // 2
    freqs = np.power(np.float32(10000.0), -np.arange(half, dtype=np.float32) / np.float32(half))
    angle = np.arange(tokens, dtype=np.float32)[:, None] * freqs[None, :].astype(np.float32)
    angle = np.tile(angle.astype(np.float64), (1, BLOCK // half))
    return np.cos(angle).astype(np.float32), np.sin(angle).astype(np.float32)


def body(
    state_tokens,
    gain_time,
    query_time,
    key_time,
    value_time,
    output_time,
    gain_space,
    query_space,
    key_space,
    value_space,
    output_space,
    neighbours,
):
    tokens, width = state_tokens.shape[1:]
    frames = lax.axis_size("frame")
    slab = 2 * BLOCK // frames
    chunks = tokens // (frames * slab)
    blocks = tokens // BLOCK
    head_dim = width // HEADS
    cosine, sine = rotary_tables(tokens, head_dim)
    vmem = pl.BlockSpec(memory_space=pltpu.VMEM)
    updated = pl.pallas_call(
        layer_kernel,
        out_shape=jax.ShapeDtypeStruct((tokens, width), BF16),
        in_specs=[pl.BlockSpec(memory_space=pltpu.SMEM)] + [vmem] * 13,
        out_specs=vmem,
        scratch_shapes=[
            pltpu.VMEM((chunks, frames, slab, width), BF16),
            pltpu.VMEM((chunks, frames, slab, width), BF16),
            pltpu.VMEM((chunks, frames, slab, width), BF16),
            pltpu.VMEM((3 * blocks, BLOCK, width), BF16),
            pltpu.VMEM((blocks, BLOCK, width), BF16),
            pltpu.VMEM((blocks, BLOCK, width), BF16),
            pltpu.VMEM((3 * blocks, BLOCK, width), BF16),
            pltpu.VMEM((3 * blocks, HEADS // 2, 2 * head_dim + 16, BLOCK), BF16),
            pltpu.VMEM((width, 2 * width), BF16),
            pltpu.VMEM((width, 2 * width), BF16),
            pltpu.VMEM((width, width), BF16),
            pltpu.VMEM((width, width), BF16),
            pltpu.VMEM((NEIGHBOUR_COUNT * BLOCK, width), BF16),
            pltpu.VMEM((NEIGHBOUR_COUNT * BLOCK, width), BF16),
            pltpu.VMEM((HEADS // 2, NEIGHBOUR_COUNT * BLOCK, 2 * BLOCK), F32),
            pltpu.VMEM((width, BLOCK), F32),
        ]
        + [pltpu.SemaphoreType.DMA((chunks,))] * 8,
        compiler_params=pltpu.CompilerParams(
            vmem_limit_bytes=48 << 20, collective_id=1, has_side_effects=True
        ),
    )(
        neighbours,
        state_tokens.reshape(tokens, width),
        gain_time.reshape(1, width),
        query_time,
        key_time,
        value_time,
        output_time,
        gain_space.reshape(1, width),
        query_space,
        key_space,
        value_space,
        output_space,
        jnp.asarray(cosine),
        jnp.asarray(sine),
    )
    return updated.reshape(state_tokens.shape)


def solution(mesh):
    return jax.shard_map(
        body,
        mesh=mesh,
        in_specs=(P("frame", "tile", None),) + (P(),) * 10 + (P("tile", None),),
        out_specs=P("frame", "tile", None),
        check_vma=False,
    )
```

time: 118 us -> 105 us (0.89)
  the two profiles are of different devices: /device:TPU:71 before, /device:TPU:384 now
where the time goes in v3:
time: 105 us; the launch traced here: 104 us
  Pallas kernels  91.7 us (87%)
  local copies, waits for them, and re-layouts  12.5 us (12%)
    pallas_call x1, Pallas kernels, body(): pl.pallas_call(layer_kernel, out_shape=jax.ShapeDtypeStruct((tokens, widt...  91.7 us
    unnamed x29, local copies, waits for them, and re-layouts  12.5 us

profile of v3, /device:TPU:384, one launch (start us, length us, event | category | flops | bytes accessed | tf_op | source)
XLA Modules:
  0.0 104.2 jit_solution(6993958166685828180)
XLA Ops:
  0.0 0.0 copy-start.11
  0.0 0.0 copy-start.12
  0.0 0.7 copy-done.11
  0.7 0.0 copy-done.12
  0.7 0.0 copy-start
  0.7 1.0 copy-done
  1.7 0.0 copy-start.1
  1.7 1.0 copy-done.1
  2.8 0.0 copy-start.2
  2.8 1.0 copy-done.2
  3.8 0.0 copy-start.3
  3.8 0.9 copy-done.3
  4.7 0.0 copy-start.4
  4.7 0.9 copy-done.4
  5.6 0.0 copy-start.5
  5.6 0.9 copy-done.5
  6.5 0.0 copy-start.6
  6.5 0.9 copy-done.6
  7.4 0.0 copy-start.7
  7.4 0.9 copy-done.7
  8.3 0.0 copy-start.8
  8.3 0.9 copy-done.8
  9.3 0.0 copy-start.9
  9.3 0.9 copy-done.9
  10.2 0.0 copy-start.10
  10.2 0.9 copy-done.10
  11.1 0.0 copy-start.13
  11.1 0.7 copy-done.13
  11.7 91.7 %shard_map.136 = bf16[1024,256]{1,0:T(8,128)(2,1)S(1)} custom-call(s32[8,9]{1,0:T(8,128)S(1)} %copy-done.11, bf16[1024,256]{1,0:T(8,128)(2,1)S(1)} %bitcast.5, f32[1,256]{1,0:T(1,128)S(1)} %bitcast.6, bf16[256,256]{1,0:T(8,128)(2,1)S(1)} %copy-done.3, bf16[256,256]{1,0:T(8,128)(2,1)S(1)} %copy-done.4, bf16[256,256]{1,0:T(8,128)(2,1)S(1)} %copy-done.5, ...), custom_call_target="tpu_custom_call" | custom-call | tf_op jit(solution)/shard_map/pallas_call | solution.py:444
  103.4 0.8 copy.16
Async XLA Ops:
  0.0 0.7 copy-start.11
  0.0 0.7 copy-start.12
  0.7 1.0 copy-start
  1.7 1.0 copy-start.1
  2.8 1.0 copy-start.2
  3.8 0.9 copy-start.3
  4.7 0.9 copy-start.4
  5.6 0.9 copy-start.5
  6.5 0.9 copy-start.6
  7.4 0.9 copy-start.7
  8.3 0.9 copy-start.8
  9.3 0.9 copy-start.9
  10.2 0.9 copy-start.10
  11.1 0.7 copy-start.13

commit v4 on v3

--- a/solution.py
+++ b/solution.py
@@ -100,6 +100,20 @@
 
 def layer_kernel(
     nbr_ref,
+    state_hbm,
+    gain_t_hbm,
+    wqt_hbm,
+    wkt_hbm,
+    wvt_in_hbm,
+    wt_hbm,
+    gain_hbm,
+    wq_hbm,
+    wk_hbm,
+    wv_hbm,
+    wo_hbm,
+    cos_hbm,
+    sin_hbm,
+    out_hbm,
     state_ref,
     gain_t_ref,
     wqt_ref,
@@ -113,7 +127,9 @@
     wo_ref,
     cos_ref,
     sin_ref,
+    load_sem,
     out_ref,
+    out_sem,
     rows_ref,
     attn_ref,
     ret_ref,
@@ -141,6 +157,12 @@
 ):
     blocks = mid_ref.shape[0]
     width = state_ref.shape[-1]
+    sources = (state_hbm, gain_t_hbm, wqt_hbm, wkt_hbm, wvt_in_hbm, wt_hbm, gain_hbm, wq_hbm, wk_hbm, wv_hbm, wo_hbm, cos_hbm, sin_hbm)
+    targets = (state_ref, gain_t_ref, wqt_ref, wkt_ref, wvt_in_ref, wt_ref, gain_ref, wq_ref, wk_ref, wv_ref, wo_ref, cos_ref, sin_ref)
+    loads = [
+        pltpu.make_async_copy(source, target, load_sem.at[i])
+        for i, (source, target) in enumerate(zip(sources, targets))
+    ]
     head_dim = width // HEADS
     scale = math.log2(math.e) / math.sqrt(head_dim)
     chunks, frames, slab, _ = rows_ref.shape
@@ -175,7 +197,7 @@
     def go(c, k):
         at = pl.ds(pl.multiple_of((c * frames + peer_at(k)) * slab, slab), slab)
         return pltpu.make_async_remote_copy(
-            src_ref=state_ref.at[at, :],
+            src_ref=state_hbm.at[at, :],
             dst_ref=rows_ref.at[c, mirror(k)],
             send_sem=go_sem.at[c],
             recv_sem=come_sem.at[c],
@@ -223,6 +245,8 @@
             device_id_type=MESH,
         )
 
+    for load in loads:
+        load.start()
     pl.semaphore_wait(barrier, frames + 1)
 
     def leave(c, carry):
@@ -233,6 +257,9 @@
         return lax.fori_loop(0, frames - 1, one, carry)
 
     lax.fori_loop(0, chunks, leave, 0)
+
+    for load in loads:
+        load.wait()
 
     def stay(c, carry):
         at = pl.ds(pl.multiple_of((c * frames + me) * slab, slab), slab)
@@ -364,6 +391,10 @@
         return carry
 
     lax.fori_loop(0, chunks, arrive, 0)
+
+    def deliver(b):
+        at = pl.ds(pl.multiple_of(b * BLOCK, BLOCK), BLOCK)
+        return pltpu.make_async_copy(out_ref.at[b], out_hbm.at[at, :], out_sem.at[b])
 
     def attend(b, tops):
         here = places(b)
@@ -385,8 +416,8 @@
         weigh(here, 3, late[1])
         early = tuple(early)
         attended = att_ref[...].T.astype(BF16)
-        at = pl.ds(pl.multiple_of(b * BLOCK, BLOCK), BLOCK)
-        out_ref[at, :] = (mid_ref[b].astype(F32) + nn(attended, wo_ref[...])).astype(BF16)
+        out_ref[b] = (mid_ref[b].astype(F32) + nn(attended, wo_ref[...])).astype(BF16)
+        deliver(b).start()
         return early
 
     at_first = places(0)
@@ -409,6 +440,12 @@
         return carry
 
     lax.fori_loop(0, chunks, sent, 0)
+
+    def delivered(b, carry):
+        deliver(b).wait()
+        return carry
+
+    lax.fori_loop(0, blocks, delivered, 0)
 
 
 def rotary_tables(tokens, head_dim):
@@ -440,13 +477,28 @@
     blocks = tokens // BLOCK
     head_dim = width // HEADS
     cosine, sine = rotary_tables(tokens, head_dim)
-    vmem = pl.BlockSpec(memory_space=pltpu.VMEM)
     updated = pl.pallas_call(
         layer_kernel,
         out_shape=jax.ShapeDtypeStruct((tokens, width), BF16),
-        in_specs=[pl.BlockSpec(memory_space=pltpu.SMEM)] + [vmem] * 13,
-        out_specs=vmem,
+        in_specs=[pl.BlockSpec(memory_space=pltpu.SMEM)] + [pl.BlockSpec(memory_space=pltpu.HBM)] * 13,
+        out_specs=pl.BlockSpec(memory_space=pltpu.HBM),
         scratch_shapes=[
+            pltpu.VMEM((tokens, width), BF16),
+            pltpu.VMEM((1, width), F32),
+            pltpu.VMEM((width, width), BF16),
+            pltpu.VMEM((width, width), BF16),
+            pltpu.VMEM((width, width), BF16),
+            pltpu.VMEM((width, width), BF16),
+            pltpu.VMEM((1, width), F32),
+            pltpu.VMEM((width, width), BF16),
+            pltpu.VMEM((width, width), BF16),
+            pltpu.VMEM((width, width), BF16),
+            pltpu.VMEM((width, width), BF16),
+            pltpu.VMEM((tokens, BLOCK), F32),
+            pltpu.VMEM((tokens, BLOCK), F32),
+            pltpu.SemaphoreType.DMA((13,)),
+            pltpu.VMEM((blocks, BLOCK, width), BF16),
+            pltpu.SemaphoreType.DMA((blocks,)),
             pltpu.VMEM((chunks, frames, slab, width), BF16),
             pltpu.VMEM((chunks, frames, slab, width), BF16),
             pltpu.VMEM((chunks, frames, slab, width), BF16),
@@ -466,7 +518,7 @@
         ]
         + [pltpu.SemaphoreType.DMA((chunks,))] * 8,
         compiler_params=pltpu.CompilerParams(
-            vmem_limit_bytes=48 << 20, collective_id=1, has_side_effects=True
+            vmem_limit_bytes=67043328, collective_id=1, has_side_effects=True
         ),
     )(
         neighbours,

time: 105 us -> 95 us (0.905)
  local copies, waits for them, and re-layouts: 12.5 us -> 1.87 us
  Pallas kernels: 91.7 us -> 92.9 us
    unnamed x29 -> x1, local copies, waits for them, and re-layouts: 12.5 us -> 1.87 us
    pallas_call x1, Pallas kernels: 91.7 us -> 92.9 us  [body(): pl.pallas_call(layer_kernel, out_shape=jax.ShapeDtypeStruct((tokens, widt...]
where the time goes in v4:
time: 95 us; the launch traced here: 94.8 us
  Pallas kernels  92.9 us (98%)
  local copies, waits for them, and re-layouts  1.87 us (2%)
    pallas_call x1, Pallas kernels, body(): pl.pallas_call(layer_kernel, out_shape=jax.ShapeDtypeStruct((tokens, widt...  92.9 us

profile of v4, /device:TPU:384, one launch (start us, length us, event | category | flops | bytes accessed | tf_op | source)
XLA Modules:
  0.0 94.8 jit_solution(7845118488997749704)
XLA Ops:
  0.0 92.9 %shard_map.136 = bf16[1024,256]{1,0:T(8,128)(2,1)} custom-call(s32[8,9]{1,0:T(8,128)} %nbr_ref.1, bf16[1024,256]{1,0:T(8,128)(2,1)} %bitcast.5, f32[1,256]{1,0:T(1,128)} %bitcast.6, bf16[256,256]{1,0:T(8,128)(2,1)} %wqt_hbm.1, bf16[256,256]{1,0:T(8,128)(2,1)} %wkt_hbm.1, bf16[256,256]{1,0:T(8,128)(2,1)} %wvt_in_hbm.1, bf16[256,256]{1,0:T(8,128)(2,1)} %wt_hbm.1, ...), custom_call_target="tpu_custom_call" | custom-call | tf_op jit(solution)/shard_map/pallas_call | solution.py:480
  92.9 1.9 %copy.16 = bf16[1,1024,256]{2,1,0:T(8,128)(2,1)} copy(bf16[1,1024,256]{2,1,0:T(8,128)(2,1)} %bitcast.4) | data formatting | bytes 1048576

commit v5 on v4

--- a/solution.py
+++ b/solution.py
@@ -324,10 +324,18 @@
                     [value_t[low : low + 2 * head_dim, k * BLOCK : (k + 1) * BLOCK], ones], axis=0
                 )
 
+    def arrive(c, carry):
+        to_left(c).wait_recv()
+        key_value(2 * blocks + per * c, per * c)
+        to_right(c).wait_recv()
+        key_value(per * c, per * c)
+        return carry
+
     gain = gain_ref[...]
 
     def own(c, carry):
         j = per * c
+        lax.fori_loop(0, jnp.where(c == chunks - 1, 1, 0), arrive, 0)
         whole(ret_ref, c, back_sem, home_sem).wait_recv()
         at = pl.ds(pl.multiple_of(c * frames * slab, frames * slab), frames * slab)
         returned = ret_ref[c].reshape(frames * slab, width)
@@ -383,14 +391,7 @@
         low = 2 * pair * head_dim
         att_ref[low : low + 2 * head_dim, :] = pair_result(nn(held, weights), head_dim, BLOCK)
 
-    def arrive(c, carry):
-        to_left(c).wait_recv()
-        key_value(2 * blocks + per * c, per * c)
-        to_right(c).wait_recv()
-        key_value(per * c, per * c)
-        return carry
-
-    lax.fori_loop(0, chunks, arrive, 0)
+    lax.fori_loop(1, chunks, arrive, 0)
 
     def deliver(b):
         at = pl.ds(pl.multiple_of(b * BLOCK, BLOCK), BLOCK)
@@ -407,12 +408,12 @@
         bias_after = bias_of(after)
         late = [score(kcb_ref, query, 2, bias)]
         weigh(here, 0, tops[0])
+        early = [score(kca_ref, query_after, 0, bias_after)]
         late.append(score(kcb_ref, query, 3, bias))
+        fill(kcb_ref, there)
         weigh(here, 1, tops[1])
-        fill(kcb_ref, there)
-        early = [score(kca_ref, query_after, 0, bias_after)]
+        early.append(score(kca_ref, query_after, 1, bias_after))
         weigh(here, 2, late[0])
-        early.append(score(kca_ref, query_after, 1, bias_after))
         weigh(here, 3, late[1])
         early = tuple(early)
         attended = att_ref[...].T.astype(BF16)
@@ -430,6 +431,7 @@
         blocks,
         attend,
         tuple(score(kca_ref, query_first, pair, bias_first) for pair in (0, 1)),
+        unroll=2,
     )
 
     def sent(c, carry):

time: 95 us -> 95.8 us (level)
  the two profiles are of different devices: /device:TPU:384 before, /device:TPU:4 now
where the time goes in v5:
time: 95.8 us; the launch traced here: 95.6 us
  Pallas kernels  93.7 us (98%)
  local copies, waits for them, and re-layouts  1.87 us (2%)
    pallas_call x1, Pallas kernels, body(): pl.pallas_call(layer_kernel, out_shape=jax.ShapeDtypeStruct((tokens, widt...  93.7 us

profile of v5, /device:TPU:4, one launch (start us, length us, event | category | flops | bytes accessed | tf_op | source)
XLA Modules:
  0.0 95.6 jit_solution(6644414004806819858)
XLA Ops:
  0.0 93.7 %shard_map.136 = bf16[1024,256]{1,0:T(8,128)(2,1)} custom-call(s32[8,9]{1,0:T(8,128)} %nbr_ref.1, bf16[1024,256]{1,0:T(8,128)(2,1)} %bitcast.5, f32[1,256]{1,0:T(1,128)} %bitcast.6, bf16[256,256]{1,0:T(8,128)(2,1)} %wqt_hbm.1, bf16[256,256]{1,0:T(8,128)(2,1)} %wkt_hbm.1, bf16[256,256]{1,0:T(8,128)(2,1)} %wvt_in_hbm.1, bf16[256,256]{1,0:T(8,128)(2,1)} %wt_hbm.1, ...), custom_call_target="tpu_custom_call" | custom-call | tf_op jit(solution)/shard_map/pallas_call | solution.py:482
  93.7 1.9 %copy.16 = bf16[1,1024,256]{2,1,0:T(8,128)(2,1)} copy(bf16[1,1024,256]{2,1,0:T(8,128)(2,1)} %bitcast.4) | data formatting | bytes 1048576

commit v6 on v4

--- a/solution.py
+++ b/solution.py
@@ -407,12 +407,12 @@
         bias_after = bias_of(after)
         late = [score(kcb_ref, query, 2, bias)]
         weigh(here, 0, tops[0])
+        early = [score(kca_ref, query_after, 0, bias_after)]
         late.append(score(kcb_ref, query, 3, bias))
+        fill(kcb_ref, there)
         weigh(here, 1, tops[1])
-        fill(kcb_ref, there)
-        early = [score(kca_ref, query_after, 0, bias_after)]
+        early.append(score(kca_ref, query_after, 1, bias_after))
         weigh(here, 2, late[0])
-        early.append(score(kca_ref, query_after, 1, bias_after))
         weigh(here, 3, late[1])
         early = tuple(early)
         attended = att_ref[...].T.astype(BF16)
@@ -430,6 +430,7 @@
         blocks,
         attend,
         tuple(score(kca_ref, query_first, pair, bias_first) for pair in (0, 1)),
+        unroll=2,
     )
 
     def sent(c, carry):

time: 95 us -> 94.5 us (level)
  no operation moved by 1% of the time
where the time goes in v6:
time: 94.5 us; the launch traced here: 94.3 us
  Pallas kernels  92.4 us (98%)
  local copies, waits for them, and re-layouts  1.87 us (2%)
    pallas_call x1, Pallas kernels, body(): pl.pallas_call(layer_kernel, out_shape=jax.ShapeDtypeStruct((tokens, widt...  92.4 us

profile of v6, /device:TPU:384, one launch (start us, length us, event | category | flops | bytes accessed | tf_op | source)
XLA Modules:
  0.0 94.3 jit_solution(15463571609736788949)
XLA Ops:
  0.0 92.4 %shard_map.136 = bf16[1024,256]{1,0:T(8,128)(2,1)} custom-call(s32[8,9]{1,0:T(8,128)} %nbr_ref.1, bf16[1024,256]{1,0:T(8,128)(2,1)} %bitcast.5, f32[1,256]{1,0:T(1,128)} %bitcast.6, bf16[256,256]{1,0:T(8,128)(2,1)} %wqt_hbm.1, bf16[256,256]{1,0:T(8,128)(2,1)} %wkt_hbm.1, bf16[256,256]{1,0:T(8,128)(2,1)} %wvt_in_hbm.1, bf16[256,256]{1,0:T(8,128)(2,1)} %wt_hbm.1, ...), custom_call_target="tpu_custom_call" | custom-call | tf_op jit(solution)/shard_map/pallas_call | solution.py:481
  92.4 1.9 %copy.16 = bf16[1,1024,256]{2,1,0:T(8,128)(2,1)} copy(bf16[1,1024,256]{2,1,0:T(8,128)(2,1)} %bitcast.4) | data formatting | bytes 1048576

commit v7 on v6

--- a/solution.py
+++ b/solution.py
@@ -254,7 +254,7 @@
             go(c, frames - 1 - i).start()
             return inner
 
-        return lax.fori_loop(0, frames - 1, one, carry)
+        return lax.fori_loop(0, frames - 1, one, carry, unroll=5)
 
     lax.fori_loop(0, chunks, leave, 0)
 
@@ -298,7 +298,7 @@
             back(c, frames - 1 - i).start()
             return inner
 
-        lax.fori_loop(0, frames - 1, one, 0)
+        lax.fori_loop(0, frames - 1, one, 0, unroll=5)
         ret_ref[c, me] = attn_ref[c, 0]
         return carry
 

time: 94.5 us -> 94.5 us (level)
  no operation moved by 1% of the time
where the time goes in v7:
time: 94.5 us; the launch traced here: 94.3 us
  Pallas kernels  92.4 us (98%)
  local copies, waits for them, and re-layouts  1.87 us (2%)
    pallas_call x1, Pallas kernels, body(): pl.pallas_call(layer_kernel, out_shape=jax.ShapeDtypeStruct((tokens, widt...  92.4 us

profile of v7, /device:TPU:384, one launch (start us, length us, event | category | flops | bytes accessed | tf_op | source)
XLA Modules:
  0.0 94.3 jit_solution(5471740249126549354)
XLA Ops:
  0.0 92.4 %shard_map.136 = bf16[1024,256]{1,0:T(8,128)(2,1)} custom-call(s32[8,9]{1,0:T(8,128)} %nbr_ref.1, bf16[1024,256]{1,0:T(8,128)(2,1)} %bitcast.5, f32[1,256]{1,0:T(1,128)} %bitcast.6, bf16[256,256]{1,0:T(8,128)(2,1)} %wqt_hbm.1, bf16[256,256]{1,0:T(8,128)(2,1)} %wkt_hbm.1, bf16[256,256]{1,0:T(8,128)(2,1)} %wvt_in_hbm.1, bf16[256,256]{1,0:T(8,128)(2,1)} %wt_hbm.1, ...), custom_call_target="tpu_custom_call" | custom-call | tf_op jit(solution)/shard_map/pallas_call | solution.py:481
  92.4 1.9 %copy.16 = bf16[1,1024,256]{2,1,0:T(8,128)(2,1)} copy(bf16[1,1024,256]{2,1,0:T(8,128)(2,1)} %bitcast.4) | data formatting | bytes 1048576
